TPU v7x, 128 devices: a whole 4x4x4 slice. The times are simulated.
128 devices in a mesh: item: 4 (over x), row: 16 (over z, y), col: 2 (over core).
Axes of the slice: x: 4, y: 4, z: 4, core: 2. Of those that a mesh axis runs over, the one named last changes fastest.
Arguments:
- img_hidden: bfloat16 [32, 1024, 3072], P('item', ('row', 'col')), parts along dimension 0, may hold values from -1.796875 to 1.796875
- text_hidden: bfloat16 [32, 512, 3072], P('item', ('row', 'col')), parts along dimension 0, may hold values from -1.796875 to 1.796875
- latent: float32 [32, 1024, 64], P('item', ('row', 'col')), parts along dimension 0, may hold values from -6 to 6
- text_len: int32 [32], P('item'), parts along dimension 0, may hold values from 1 to 512, as said below
- block_keep: int32 [32, 16], P('item'), parts along dimension 0, may hold values 0 or 1
- img_pos: int32 [1024, 3], P(('row', 'col')), may hold values from 0 to 62, as said below
- modulation: float32 [32, 5, 3072], P('item'), parts along dimension 0, may hold values from -4 to 4
- qk_gain: float32 [2, 128], replicated, may hold values from 0.7 to 7
- w_qkv: bfloat16 [3072, 3, 1536], P(None, None, 'col'), may hold values from -0.109375 to 0.109375
- w_out: bfloat16 [1536, 3072], P('col'), may hold values from -0.25 to 0.25
- w_final: bfloat16 [3072, 64], replicated, may hold values from -0.109375 to 0.109375
Outputs:
- img_out: bfloat16 [32, 1024, 3072], P('item', ('row', 'col')), parts along dimension 0
- text_out: bfloat16 [32, 512, 3072], P('item', ('row', 'col')), parts along dimension 0
- latent_next: float32 [32, 1024, 64], P('item', ('row', 'col')), parts along dimension 0
There are 4 independent parts, one for each index of `item`. A program takes and returns all parts, laid end to end along the dimension named above; an argument that names none is the same for every part. Nothing has to cross between parts.
Inputs may be any that keep to these rules, and one draw needn't show every extreme that they name: `text_len`: at least one sample of every request uses all 512 text slots. `img_pos`: image token i, in image row r = i // 32 and column q = i % 32, has ids (c_i, a_r + r, b_q + q), where every token has its own frame id c_i of 0 to 3, every image row its own offset a_r and every image column its own offset b_q, each of 0 to 31.
All inputs are finite; a program needn't handle non-finite values.
Results may differ from a plain program's by a relative error of at most 0.015.
The roundings to bfloat16 on the way count: a program that leaves them out, or rounds other values in their place, can miss the bound.
Values may be sent and summed in bfloat16 or wider, within the bound.
No kernel may reach another device: no remote copies, remote signals or barrier semaphores. Data moves between devices by JAX's collectives and lax.ppermute only.
A program may use at most 256 MiB of HBM per device.

v0:
```python
import jax
import jax.numpy as jnp
import numpy as np
from jax import lax
from jax.sharding import PartitionSpec as P

KBLK = 64


eps_norm = 1e-06
theta_base = 10000.0
step_size = -0.25


def layer_norm(values):
    center = values - jnp.mean(values, axis=-1, keepdims=True)
    return center * lax.rsqrt(jnp.mean(center * center, axis=-1, keepdims=True) + eps_norm)


def modulate(hidden, shift, scale):
    return ((1.0 + scale) * layer_norm(hidden.astype(jnp.float32)) + shift).astype(jnp.bfloat16)


def rope_tables(head_dim):
    half = head_dim // 2
    first = head_dim // 16
    second = (half - first) // 2
    counts = [first, second, half - first - second]
    tables = []
    for axis_id in range(3):
        pieces = []
        for other in range(3):
            if other == axis_id:
                pieces.append(theta_base ** (-np.arange(counts[other]) / counts[other]))
            else:
                pieces.append(np.zeros(counts[other]))
        tables.append(np.concatenate(pieces).astype(np.float32))
    return tables


def angles_of(positions, head_dim):
    tables = rope_tables(head_dim)
    angle = positions[:, 0:1] * jnp.asarray(tables[0]) + positions[:, 1:2] * jnp.asarray(tables[1])
    angle = angle + positions[:, 2:3] * jnp.asarray(tables[2])
    return (jnp.cos(angle), jnp.sin(angle))


def rotate(values, cosine, sine):
    half = values.shape[-1] // 2
    first_half = values[..., :half]
    second_half = values[..., half:]
    cos_rows = cosine[:, None, :]
    sin_rows = sine[:, None, :]
    return jnp.concatenate(
        [
            first_half * cos_rows - second_half * sin_rows,
            second_half * cos_rows + first_half * sin_rows,
        ],
        axis=-1,
    )


def rms_gain(values, gain):
    return values * lax.rsqrt(jnp.mean(values * values, axis=-1, keepdims=True) + eps_norm) * gain


def valid_keys(text_len, block_keep, count, text_rows, img_rows):
    group = text_rows + img_rows
    index = jnp.arange(count, dtype=jnp.int32)
    device = index // group
    local = index % group
    is_text = local < text_rows
    text_index = device * text_rows + local
    img_index = device * img_rows + jnp.maximum(local - text_rows, 0)
    text_ok = text_index[None, :] < text_len[:, None]
    onehot = (
        (img_index // KBLK)[:, None] == jnp.arange(block_keep.shape[1], dtype=jnp.int32)[None, :]
    ).astype(jnp.int32)
    img_ok = jnp.sum(block_keep[:, None, :] * onehot[None], axis=-1) > 0
    return jnp.where(is_text[None, :], text_ok, img_ok)


def absorb(state, piece, valid, query):
    top, total, summed = state
    key_piece, value_piece = piece
    samples = key_piece.shape[0]
    count = key_piece.shape[1]
    heads = query.shape[2]
    head_dim = query.shape[3]
    key_split = key_piece.reshape(samples, count, heads, head_dim)
    value_split = value_piece.reshape(samples, count, heads, head_dim)
    scores = jnp.einsum(
        "sqhd,skhd->shqk", query, key_split, preferred_element_type=jnp.float32
    ) * head_dim ** (-0.5)
    scores = jnp.where(valid[:, None, None, :], scores, -jnp.inf)
    new_top = jnp.maximum(top, jnp.max(scores, axis=-1))
    weights = jnp.exp(scores - new_top[..., None])
    factor = jnp.exp(top - new_top)
    total = total * factor + jnp.sum(weights, axis=-1)
    summed = summed * factor[..., None] + jnp.einsum(
        "shqk,skhd->shqd",
        weights.astype(jnp.bfloat16),
        value_split,
        preferred_element_type=jnp.float32,
    )
    return (new_top, total, summed)


def per_device(
    img_hidden,
    text_hidden,
    latent,
    text_len,
    block_keep,
    img_pos,
    modulation,
    qk_gain,
    w_qkv,
    w_out,
    w_final,
):
    samples = img_hidden.shape[0]
    width = img_hidden.shape[2]
    head_dim = qk_gain.shape[1]
    local_inner = w_out.shape[0]
    local_heads = local_inner // head_dim
    mod_rows = modulation[:, :, None, :]
    text_norm = modulate(text_hidden, mod_rows[:, 0], mod_rows[:, 1])
    img_norm = modulate(img_hidden, mod_rows[:, 0], mod_rows[:, 1])
    text_group, img_group, pos_group = (
        lax.all_gather(text_norm, "col", axis=1, tiled=True),
        lax.all_gather(img_norm, "col", axis=1, tiled=True),
        lax.all_gather(img_pos.astype(jnp.bfloat16), "col", axis=0, tiled=True),
    )
    text_rows = text_group.shape[1]
    img_rows = img_group.shape[1]
    group = text_rows + img_rows
    joined = jnp.concatenate([text_group, img_group], axis=1)
    mixed = jnp.dot(
        joined.reshape(samples * group, width),
        w_qkv.reshape(width, 3 * local_inner),
        preferred_element_type=jnp.float32,
    )
    mixed = mixed.reshape(samples, group, 3, local_heads, head_dim)
    positions = jnp.concatenate(
        [jnp.zeros((text_rows, 3), jnp.float32), pos_group.astype(jnp.float32)], axis=0
    )
    cosine, sine = angles_of(positions, head_dim)
    query = rotate(rms_gain(mixed[:, :, 0], qk_gain[0]), cosine, sine).astype(jnp.bfloat16)
    keys = (
        rotate(rms_gain(mixed[:, :, 1], qk_gain[1]), cosine, sine)
        .astype(jnp.bfloat16)
        .reshape(samples, group, local_inner)
    )
    values = mixed[:, :, 2].astype(jnp.bfloat16).reshape(samples, group, local_inner)
    start_state = (
        jnp.full((samples, local_heads, group), -1e30, jnp.float32),
        jnp.zeros((samples, local_heads, group), jnp.float32),
        jnp.zeros((samples, local_heads, group, head_dim), jnp.float32),
    )
    piece = (
        lax.all_gather(keys, "row", axis=1, tiled=True),
        lax.all_gather(values, "row", axis=1, tiled=True),
    )
    count = piece[0].shape[1]
    valid = valid_keys(text_len, block_keep, count, text_rows, img_rows)
    top, total, summed = absorb(start_state, piece, valid, query)
    attention = jnp.transpose(summed / total[..., None], (0, 2, 1, 3)).astype(jnp.bfloat16)
    attention = attention.reshape(samples, group, local_inner)
    partial_sum = jnp.dot(
        attention.reshape(samples * group, local_inner), w_out, preferred_element_type=jnp.float32
    )
    partial_sum = partial_sum.reshape(samples, group, width)
    text_sum, img_sum = (
        lax.psum_scatter(
            partial_sum[:, :text_rows].astype(jnp.bfloat16), "col", scatter_dimension=1, tiled=True
        ).astype(jnp.float32),
        lax.psum_scatter(
            partial_sum[:, text_rows:].astype(jnp.bfloat16), "col", scatter_dimension=1, tiled=True
        ).astype(jnp.float32),
    )
    text_out = (text_hidden.astype(jnp.float32) + mod_rows[:, 2] * text_sum).astype(jnp.bfloat16)
    img_out = (img_hidden.astype(jnp.float32) + mod_rows[:, 2] * img_sum).astype(jnp.bfloat16)
    final = modulate(img_out, mod_rows[:, 3], mod_rows[:, 4])
    velocity = jnp.dot(
        final.reshape(samples * img_hidden.shape[1], width),
        w_final,
        preferred_element_type=jnp.float32,
    )
    velocity = velocity.reshape(samples, img_hidden.shape[1], w_final.shape[1])
    return (img_out, text_out, latent + step_size * velocity)


def solution(mesh):
    placed = (
        P("item", ("row", "col"), None),
        P("item", ("row", "col"), None),
        P("item", ("row", "col"), None),
        P("item"),
        P("item", None),
        P(("row", "col"), None),
        P("item", None, None),
        P(),
        P(None, None, "col"),
        P("col", None),
        P(),
    )
    return jax.shard_map(
        per_device,
        mesh=mesh,
        in_specs=placed,
        out_specs=(
            P("item", ("row", "col"), None),
            P("item", ("row", "col"), None),
            P("item", ("row", "col"), None),
        ),
        check_vma=False,
    )
```

profile of v0, /device:TPU:0, one launch (start us, length us, event | category | flops | bytes accessed | tf_op | source)
XLA Modules:
  0.0 408.6 jit_solution(13633441374526397716)
XLA Ops:
  7.2 1.3 fusion.55
  8.5 1.3 convert_reduce_fusion.2
  9.8 1.5 fusion.32
  11.3 1.3 fusion.35
  13.6 2.0 fusion.20
  15.7 18.7 %copy.38 = bf16[3072,3,768]{0,2,1:T(8,128)(2,1)} copy(bf16[3072,3,768]{2,0,1:T(8,128)(2,1)} %param.22) | data formatting | bytes 28311552 | tf_op args[8]
  34.4 1.8 all-gather
  36.7 9.4 %all-gather.8.cloned.1.call-done = bf16[8,64,3072]{2,1,0:T(8,128)(2,1)} async-done(((bf16[8,32,3072]{2,1,0:T(8,128)(2,1)}), bf16[8,64,3072]{2,1,0:T(8,128)(2,1)}) %all-gather.8.cloned.1.call-update) | async-done | bytes 3145744 | tf_op jit(solution)/shard_map/all_gather | solution.py:132
  46.2 14.7 %fusion.9 = f32[8,96,3,6,128]{4,1,3,2,0:T(8,128)S(1)} fusion(bf16[3,6,128,3072,1]{3,2,1,0,4:T(8,128)(2,1)} %bitcast.90, bf16[8,64,3072]{2,1,0:T(8,128)(2,1)} %all-gather.8.cloned.1.call-done, bf16[8,32,3072]{2,1,0:T(8,128)(2,1)} %all-gather.6.cloned.1.call-done), kind=kOutput, calls=%fused_computation.15 | convolution fusion | flops 10881073152 | bytes 25952256 | tf_op jit(solution)/shard_map/dot_general | solution.py:139
  60.9 1.7 multiply_reduce_fusion.1
  62.7 1.5 multiply_multiply_fusion.1
  64.2 2.8 subtract_convert_fusion.1
  67.0 1.6 copy_bitcast_fusion
  68.7 1.8 slice.129
  70.5 1.7 copy.44
  72.2 3.8 convert_element_type.70
  76.7 115.6 %all-gather.10.cloned.1.call-done = bf16[8,1536,768]{2,1,0:T(8,128)(2,1)} async-done(((bf16[8,96,768]{2,1,0:T(8,128)(2,1)}), bf16[8,1536,768]{2,1,0:T(8,128)(2,1)}) %all-gather.10.cloned.1.call-update) | async-done | bytes 18874384 | tf_op jit(solution)/shard_map/all_gather | solution.py:162
  192.3 24.8 %copy.42 = bf16[8,1536,768]{1,2,0:T(8,128)(2,1)} copy(bf16[8,1536,768]{2,1,0:T(8,128)(2,1)} %all-gather.10.cloned.1.call-done) | data formatting | bytes 37748736 | tf_op jit(solution)/shard_map/all_gather | solution.py:162
  217.1 16.8 %fusion = (f32[8,6,96]{2,1,0:T(8,128)S(1)}, f32[8,6,96,1536]{3,2,1,0:T(8,128)}) fusion(pred[8,1536]{1,0:T(8,128)(4,1)S(1)} %compare_select_fusion, bf16[8,1536,6,128]{1,3,2,0:T(8,128)(2,1)} %bitcast.88, bf16[8,96,6,64]{3,1,2,0:T(8,128)(2,1)} %get-tuple-element.10, bf16[8,96,6,64]{3,1,2,0:T(8,128)(2,1)} %get-tuple-element.9), kind=kOutput, calls=%fused_computation.2 | convolution fusion | flops 1835527680 | bytes 48396288 | tf_op jit(solution)/shard_map/sqhd,skhd->shqk/dot_general | solution.py:92
  233.9 11.8 %fusion.1 = f32[8,6,96]{2,1,0:T(8,128)S(1)} fusion(f32[8,6,96,1536]{3,2,1,0:T(8,128)} %get-tuple-element.30, f32[8,6,96]{2,1,0:T(8,128)S(1)} %get-tuple-element.21, pred[8,1536]{1,0:T(8,128)(4,1)S(1)} %compare_select_fusion), kind=kLoop, calls=%fused_computation.3 | loop fusion | flops 28306944 | bytes 28360704 | tf_op jit(solution)/shard_map/reduce_sum | solution.py:99
  245.7 70.4 %all-gather.12.cloned.1.call-done = bf16[8,1536,768]{2,1,0:T(8,128)(2,1)} async-done(((bf16[8,96,768]{2,1,0:T(8,128)(2,1)}), bf16[8,1536,768]{2,1,0:T(8,128)(2,1)}) %all-gather.12.cloned.1.call-update) | async-done | bytes 18874384 | tf_op jit(solution)/shard_map/all_gather | solution.py:163
  316.1 24.7 %copy.45 = bf16[8,1536,768]{1,2,0:T(8,128)(2,1)} copy(bf16[8,1536,768]{2,1,0:T(8,128)(2,1)} %all-gather.12.cloned.1.call-done) | data formatting | bytes 37748736 | tf_op jit(solution)/shard_map/all_gather | solution.py:163
  340.8 18.1 %fusion.39 = bf16[8,6,12,8,128]{4,3,2,1,0:T(8,128)(2,1)} fusion(bf16[8,1536,6,128]{1,3,2,0:T(8,128)(2,1)} %bitcast.89, f32[8,6,96,1536]{3,2,1,0:T(8,128)} %get-tuple-element.30, f32[8,6,96]{2,1,0:T(8,128)S(1)} %get-tuple-element.21, pred[8,1536]{1,0:T(8,128)(4,1)S(1)} %compare_select_fusion, f32[8,96,6]{1,2,0:T(8,128)S(1)} %bitcast_add_fusion.1, ...), kind=kOutput, calls=%fused_computation.59 | convolution fusion | flops 1842020352 | bytes 48433152 | tf_op jit(solution)/shard_map/shqk,skhd->shqd/dot_general | solution.py:100
  358.8 6.5 %convolution_convert_fusion = bf16[8,96,3072]{2,1,0:T(8,128)(2,1)S(1)} fusion(bf16[768,3072]{1,0:T(8,128)(2,1)} %param.23, bf16[8,6,12,8,128]{4,3,2,1,0:T(8,128)(2,1)} %fusion.39), kind=kOutput, calls=%fused_computation.10 | convolution fusion | flops 3626237952 | bytes 10616832 | tf_op jit(solution)/shard_map/dot_general | solution.py:170
  365.4 2.1 copy-done.5
  367.5 1.2 slice.93
  369.0 3.8 slice.92
  372.8 7.3 %reduce-scatter.5.cloned.1.call-done = bf16[8,16,3072]{2,1,0:T(8,128)(2,1)} async-done(((bf16[8,32,3072]{2,1,0:T(8,128)(2,1)}), bf16[8,16,3072]{2,1,0:T(8,128)(2,1)}) %reduce-scatter.5.cloned.1.call-update) | async-done | bytes 786448 | tf_op jit(solution)/shard_map/reduce_scatter | solution.py:175
  380.2 2.2 fusion.36
  382.4 15.1 %reduce-scatter.3.cloned.1.call-done = bf16[8,32,3072]{2,1,0:T(8,128)(2,1)} async-done(((bf16[8,64,3072]{2,1,0:T(8,128)(2,1)}), bf16[8,32,3072]{2,1,0:T(8,128)(2,1)}) %reduce-scatter.3.cloned.1.call-update) | async-done | bytes 1572880 | tf_op jit(solution)/shard_map/reduce_scatter | solution.py:178
  397.5 2.1 convert_reduce_fusion.1
  400.3 1.5 fusion.51
  (65 shorter events, 3.2 us)
Async XLA Ops:
  7.2 393.1 %copy-start = (bf16[3072,64]{0,1:T(8,128)(2,1)S(1)}, bf16[3072,64]{0,1:T(8,128)(2,1)}, u32[]{:S(2)}) copy-start(bf16[3072,64]{0,1:T(8,128)(2,1)} %param.24) | copy-start | bytes 1179652
  7.2 4.1 %copy-start.3 = (bf16[8,16,3072]{2,1,0:T(8,128)(2,1)S(1)}, bf16[8,16,3072]{2,1,0:T(8,128)(2,1)}, u32[]{:S(2)}) copy-start(bf16[8,16,3072]{2,1,0:T(8,128)(2,1)} %param.15) | copy-start | bytes 2359300
  7.2 29.5 %all-gather.6.cloned.1.call-start = ((), (), s32[]{:S(2)}) async-start(), calls=%async_computation.2 | async-start | bytes 2359296 | tf_op jit(solution)/shard_map/all_gather | solution.py:131
  7.2 5.5 %copy-start.1 = (bf16[8,32,3072]{2,1,0:T(8,128)(2,1)S(1)}, bf16[8,32,3072]{2,1,0:T(8,128)(2,1)}, u32[]{:S(2)}) copy-start(bf16[8,32,3072]{2,1,0:T(8,128)(2,1)} %param.14) | copy-start | bytes 4718596
  12.7 33.5 %all-gather.8.cloned.1.call-start = ((), (), s32[]{:S(2)}) async-start(), calls=%async_computation.3 | async-start | bytes 4718592 | tf_op jit(solution)/shard_map/all_gather | solution.py:132
  15.6 18.9 %copy-start.7 = (s32[32,3]{0,1:T(4,128)S(1)}, s32[32,3]{0,1:T(4,128)}, u32[]{:S(2)}) copy-start(s32[32,3]{0,1:T(4,128)} %param.19) | copy-start | bytes 1156
  15.6 20.8 %copy-start.8 = (f32[2,128]{1,0:T(2,128)S(1)}, f32[2,128]{1,0:T(2,128)}, u32[]{:S(2)}) copy-start(f32[2,128]{1,0:T(2,128)} %param.21) | copy-start | bytes 3076
  15.6 20.8 %copy-start.10 = (f32[64]{0:T(128)S(1)}, f32[64]{0:T(128)}, u32[]{:S(2)}) copy-start(f32[64]{0:T(128)} %constant.80.clone) | copy-start | bytes 772
  15.6 20.8 %copy-start.11 = (f32[64]{0:T(128)S(1)}, f32[64]{0:T(128)}, u32[]{:S(2)}) copy-start(f32[64]{0:T(128)} %constant.81.clone) | copy-start | bytes 772
  15.6 20.8 %copy-start.12 = (f32[64]{0:T(128)S(1)}, f32[64]{0:T(128)}, u32[]{:S(2)}) copy-start(f32[64]{0:T(128)} %constant.82.clone) | copy-start | bytes 772
  15.6 176.7 %all-gather.10.cloned.1.call-start = ((), (), s32[]{:S(2)}) async-start(), calls=%async_computation.4 | async-start | bytes 20054016 | tf_op jit(solution)/shard_map/all_gather | solution.py:162
  60.9 3.3 copy-start.2
  68.6 247.5 %all-gather.12.cloned.1.call-start = ((), (), s32[]{:S(2)}) async-start(), calls=%async_computation.5 | async-start | bytes 20054016 | tf_op jit(solution)/shard_map/all_gather | solution.py:163
  72.2 4.2 %copy-start.6 = (s32[8,16]{1,0:T(8,128)S(1)}, s32[8,16]{1,0:T(8,128)}, u32[]{:S(2)}) copy-start(s32[8,16]{1,0:T(8,128)} %param.18) | copy-start | bytes 1540
  72.2 4.4 %copy-start.9 = (s32[8]{0:T(128)S(1)}, s32[8]{0:T(128)}, u32[]{:S(2)}) copy-start(s32[8]{0:T(128)} %param.17) | copy-start | bytes 100
  76.0 304.1 %reduce-scatter.5.cloned.1.call-start = ((), (), s32[]{:S(2)}) async-start(), calls=%async_computation.7 | async-start | bytes 2359296 | tf_op jit(solution)/shard_map/reduce_scatter | solution.py:175
  365.4 2.1 copy-start.5
  368.8 28.8 %reduce-scatter.3.cloned.1.call-start = ((), (), s32[]{:S(2)}) async-start(), calls=%async_computation.6 | async-start | bytes 4718592 | tf_op jit(solution)/shard_map/reduce_scatter | solution.py:178
  382.4 17.9 %copy-start.13 = (f32[8,32,64]{2,1,0:T(8,128)S(1)}, f32[8,32,64]{2,1,0:T(8,128)}, u32[]{:S(2)}) copy-start(f32[8,32,64]{2,1,0:T(8,128)} %param.16) | copy-start | bytes 196612
  399.7 2.1 copy-start.4
Sparse Core Ops, SparseCore 0:
  12.8 14.9 all-gather.5
  30.0 16.1 all-gather.7
  68.7 123.5 all-gather.9
  194.3 121.7 all-gather.11
  368.9 11.2 reduce-scatter.4
  382.5 14.9 reduce-scatter.2
where the time goes:
time: 412 us; the launch traced here: 409 us
  waiting for transfers between devices  218 us (53%)
  local copies, waits for them, and re-layouts  82.9 us (20%)
  matrix products  57.6 us (14%)
  other arithmetic  33.3 us (8%)
  between operations  14.4 us (3%)
    all_gather x1, waiting for transfers between devices, per_device(): lax.all_gather(keys, 'row', axis=1, tiled=True)  116 us
    all_gather x1, waiting for transfers between devices, per_device(): lax.all_gather(values, 'row', axis=1, tiled=True)  70.4 us
    all_gather x1, local copies, waits for them, and re-layouts, per_device(): lax.all_gather(keys, 'row', axis=1, tiled=True)  24.8 us
    all_gather x1, local copies, waits for them, and re-layouts, per_device(): lax.all_gather(values, 'row', axis=1, tiled=True)  24.7 us
    unnamed x30, local copies, waits for them, and re-layouts  21 us
    dot_general x1, matrix products, absorb(): jnp.einsum('shqk,skhd->shqd', weights.astype(jnp.bfloat16), value_split,...  18.1 us
    dot_general x1, matrix products, absorb(): jnp.einsum('sqhd,skhd->shqk', query, key_split, preferred_element_type=jn...  16.8 us
    reduce_scatter x1, waiting for transfers between devices, per_device(): lax.psum_scatter(partial_sum[:, text_rows:].astype(jnp.bfloat16), 'col',...  15.1 us
  transfers between devices with their start and end apart: 6, of which 5 were waited for; matrix products, arithmetic and copies ran while one was open for 22% of the time, Pallas kernels for 0%

commit v1 on v0

v1 whole, which is shorter than its diff:
```python
import functools
import math

import jax
import jax.numpy as jnp
import numpy as np
from jax import lax
from jax.experimental import pallas as pl
from jax.experimental.pallas import tpu as pltpu
from jax.sharding import PartitionSpec as P

eps_norm = 1e-06
theta_base = 10000.0
step_size = -0.25
MIB = 1 << 20
F32 = jnp.float32
BF16 = jnp.bfloat16


def rope_rates(head_dim):
    half = head_dim // 2
    first = head_dim // 16
    second = (half - first) // 2
    counts = [first, second, half - first - second]
    tables = []
    for axis_id in range(3):
        pieces = []
        for other in range(3):
            if other == axis_id:
                pieces.append(theta_base ** (-np.arange(counts[other]) / counts[other]))
            else:
                pieces.append(np.zeros(counts[other]))
        tables.append(np.concatenate(pieces).astype(np.float32))
    return tables


def rope_tables(img_pos, text_rows, head_dim):
    tables = rope_rates(head_dim)
    pos = img_pos.astype(F32)
    angle = pos[:, 0:1] * tables[0] + pos[:, 1:2] * tables[1]
    angle = angle + pos[:, 2:3] * tables[2]
    half = head_dim // 2
    cosine = jnp.concatenate([jnp.ones((text_rows, half), F32), jnp.cos(angle)], axis=0)
    sine = jnp.concatenate([jnp.zeros((text_rows, half), F32), jnp.sin(angle)], axis=0)
    return (
        jnp.concatenate([cosine, cosine], axis=1),
        jnp.concatenate([-sine, sine], axis=1),
    )


def layer_norm(values):
    center = values - jnp.mean(values, axis=-1, keepdims=True)
    return center * lax.rsqrt(jnp.mean(center * center, axis=-1, keepdims=True) + eps_norm)


def norm_kernel(text_ref, img_ref, mod_ref, out_ref):
    s = pl.program_id(0)
    text_rows = text_ref.shape[1]
    shift = mod_ref[0, pl.ds(s, 1), :]
    scale = 1.0 + mod_ref[1, pl.ds(s, 1), :]
    out_ref[0, :text_rows] = (scale * layer_norm(text_ref[0].astype(F32)) + shift).astype(BF16)
    out_ref[0, text_rows:] = (scale * layer_norm(img_ref[0].astype(F32)) + shift).astype(BF16)


def norm_tokens(text_hidden, img_hidden, mod):
    samples, text_rows, width = text_hidden.shape
    img_rows = img_hidden.shape[1]
    rows = text_rows + img_rows
    return pl.pallas_call(
        norm_kernel,
        grid=(samples,),
        in_specs=[
            pl.BlockSpec((1, text_rows, width), lambda s: (s, 0, 0)),
            pl.BlockSpec((1, img_rows, width), lambda s: (s, 0, 0)),
            pl.BlockSpec((2, samples, width), lambda s: (0, 0, 0)),
        ],
        out_specs=pl.BlockSpec((1, rows, width), lambda s: (s, 0, 0)),
        out_shape=jax.ShapeDtypeStruct((samples, rows, width), BF16),
        compiler_params=pltpu.CompilerParams(vmem_limit_bytes=16 * MIB),
        cost_estimate=pl.CostEstimate(
            flops=samples * rows * width * 10,
            bytes_accessed=samples * rows * width * 4,
            transcendentals=0,
        ),
        name="norm_tokens",
    )(text_hidden, img_hidden, mod)


def qkv_kernel(col_ref, own_ref, other_ref, w_ref, rope_ref, gain_ref, out_ref):
    t = pl.program_id(1)
    samples, rows, width = own_ref.shape
    head_dim = gain_ref.shape[1]
    col = col_ref[0]

    def project(x_ref, half, place, rotated):
        y = jnp.dot(
            x_ref[...].reshape(samples * rows, width), w_ref[0], preferred_element_type=F32
        )
        for hh in range(2):
            v = y[:, hh * head_dim : (hh + 1) * head_dim]
            if rotated:
                v = v * lax.rsqrt(jnp.mean(v * v, axis=-1, keepdims=True) + eps_norm)
                v = v * gain_ref[pl.ds(t, 1), :]
                v3 = v.reshape(samples, rows, head_dim)
                r3 = pltpu.roll(v, head_dim // 2, 1).reshape(samples, rows, head_dim)
                v3 = v3 * rope_ref[half, 0][None] + r3 * rope_ref[half, 1][None]
            else:
                v3 = v.reshape(samples, rows, head_dim)
            out_ref[:, hh, place] = v3.astype(BF16)

    for half, x_ref in ((0, own_ref), (1, other_ref)):
        place = col if half == 0 else 1 - col

        @pl.when(t < 2)
        def _(x_ref=x_ref, half=half, place=place):
            project(x_ref, half, place, True)

        @pl.when(t == 2)
        def _(x_ref=x_ref, half=half, place=place):
            project(x_ref, half, place, False)


def qkv_heads(col, own, other, w_qkv, rope, gain, first, count):
    samples, rows, width = own.shape
    head_dim = gain.shape[1]
    return pl.pallas_call(
        qkv_kernel,
        grid_spec=pltpu.PrefetchScalarGridSpec(
            num_scalar_prefetch=1,
            grid=(count, 3),
            in_specs=[
                pl.BlockSpec((samples, rows, width), lambda j, t, c: (0, 0, 0)),
                pl.BlockSpec((samples, rows, width), lambda j, t, c: (0, 0, 0)),
                pl.BlockSpec((1, width, 2 * head_dim), lambda j, t, c: (t, 0, first + j)),
                pl.BlockSpec(rope.shape, lambda j, t, c: (0, 0, 0, 0)),
                pl.BlockSpec(gain.shape, lambda j, t, c: (0, 0)),
            ],
            out_specs=pl.BlockSpec(
                (samples, 2, 2, rows, head_dim), lambda j, t, c: (0, 0, 0, 0, 3 * j + t)
            ),
        ),
        out_shape=jax.ShapeDtypeStruct((samples, 2, 2, rows, 3 * count * head_dim), BF16),
        compiler_params=pltpu.CompilerParams(vmem_limit_bytes=32 * MIB),
        cost_estimate=pl.CostEstimate(
            flops=2 * samples * 2 * rows * width * 6 * count * head_dim,
            bytes_accessed=2 * (2 * samples * rows * width + width * 6 * count * head_dim),
            transcendentals=0,
        ),
        name="qkv_heads",
    )(col, own, other, w_qkv, rope, gain)


def attend_kernel(q_ref, k_ref, v_ref, bias_ref, *refs):
    out_ref = refs[-1]
    head_dim = q_ref.shape[1]
    factor = math.log2(math.e) / math.sqrt(head_dim)
    scores = lax.dot_general(
        q_ref[...], k_ref[...], (((1,), (1,)), ((), ())), preferred_element_type=F32
    )
    scores = scores * factor + bias_ref[...]
    top = jnp.max(scores, axis=-1, keepdims=True)
    weights = jnp.exp2(scores - top)
    total = jnp.sum(weights, axis=-1, keepdims=True)
    summed = jnp.dot(weights.astype(BF16), v_ref[...], preferred_element_type=F32)
    out_ref[...] = (summed / total).astype(BF16)


def attend(packed, bias, before, head_dim, block, first, heads):
    tokens = packed.shape[0]
    count = packed.shape[1] // (3 * head_dim)
    operands = [packed, packed, packed, bias]
    in_specs = [
        pl.BlockSpec((block, head_dim), lambda j, i: (i, 3 * j)),
        pl.BlockSpec((tokens, head_dim), lambda j, i: (0, 3 * j + 1)),
        pl.BlockSpec((tokens, head_dim), lambda j, i: (0, 3 * j + 2)),
        pl.BlockSpec((1, tokens), lambda j, i: (0, 0)),
    ]
    if before is not None:
        operands.append(before)
        in_specs.append(pl.BlockSpec(memory_space=pl.ANY))
    return pl.pallas_call(
        attend_kernel,
        grid=(count, tokens // block),
        in_specs=in_specs,
        out_specs=pl.BlockSpec((block, head_dim), lambda j, i: (i, first + j)),
        out_shape=jax.ShapeDtypeStruct((tokens, heads * head_dim), BF16),
        input_output_aliases={} if before is None else {4: 0},
        compiler_params=pltpu.CompilerParams(vmem_limit_bytes=32 * MIB),
        cost_estimate=pl.CostEstimate(
            flops=4 * count * tokens * tokens * head_dim,
            bytes_accessed=2 * 4 * count * tokens * head_dim,
            transcendentals=count * tokens * tokens,
        ),
        name="attend",
    )(*operands)


def finish_kernel(
    col_ref, att_ref, own_w_ref, other_w_ref, text_ref, img_ref, mod_ref, wf_ref,
    latent_ref, text_out_ref, img_out_ref, next_ref, acc, final
):
    hh = pl.program_id(0)
    side = pl.program_id(1)
    samples, text_rows, width = text_ref.shape
    img_rows = img_ref.shape[1]
    rows = text_rows + img_rows

    def add(w_ref):
        lhs = att_ref[...].reshape(samples * rows, att_ref.shape[-1])
        return jnp.dot(lhs, w_ref[...].reshape(-1, width), preferred_element_type=F32)

    @pl.when((hh == 0) & (side == 0))
    def _():
        acc[...] = add(own_w_ref)

    @pl.when((hh == 1) & (side == 0))
    def _():
        acc[...] += add(own_w_ref)

    @pl.when(side == 1)
    def _():
        acc[...] += add(other_w_ref)

    @pl.when((hh == 1) & (side == 1))
    def _():
        def sample(s, carry):
            start = pl.multiple_of(s * rows, 16)
            gate = mod_ref[2, pl.ds(s, 1), :]
            text_sum = acc[pl.ds(start, text_rows), :]
            text_out_ref[s] = (text_ref[s].astype(F32) + gate * text_sum).astype(BF16)
            img_sum = acc[pl.ds(start + text_rows, img_rows), :]
            img = (img_ref[s].astype(F32) + gate * img_sum).astype(BF16)
            img_out_ref[s] = img
            normed = layer_norm(img.astype(F32))
            scaled = (1.0 + mod_ref[4, pl.ds(s, 1), :]) * normed + mod_ref[3, pl.ds(s, 1), :]
            final[pl.ds(pl.multiple_of(s * img_rows, 16), img_rows), :] = scaled.astype(BF16)
            return carry

        lax.fori_loop(0, samples, sample, 0)
        velocity = lax.dot_general(
            final[...], wf_ref[...], (((1,), (1,)), ((), ())), preferred_element_type=F32
        )
        next_ref[...] = latent_ref[...] + step_size * velocity.reshape(latent_ref.shape)


def finish(col, att, own_w, other_w, text_hidden, img_hidden, mod, w_final, latent):
    samples, text_rows, width = text_hidden.shape
    img_rows = img_hidden.shape[1]
    rows = text_rows + img_rows
    groups = own_w.shape[0]
    head_dim = own_w.shape[2]
    whole = lambda shape: pl.BlockSpec(shape, lambda h, o, c: (0,) * len(shape))
    att_spec = pl.BlockSpec(
        (samples, None, None, rows, att.shape[-1]),
        lambda h, o, c: (0, h, c[0] + o - 2 * c[0] * o, 0, 0),
    )
    w_spec = pl.BlockSpec((groups, None, head_dim, width), lambda h, o, c: (0, h, 0, 0))
    return pl.pallas_call(
        finish_kernel,
        grid_spec=pltpu.PrefetchScalarGridSpec(
            num_scalar_prefetch=1,
            grid=(2, 2),
            in_specs=[
                att_spec,
                w_spec,
                w_spec,
                whole(text_hidden.shape),
                whole(img_hidden.shape),
                whole(mod.shape),
                whole(w_final.shape),
                whole(latent.shape),
            ],
            out_specs=[whole(text_hidden.shape), whole(img_hidden.shape), whole(latent.shape)],
            scratch_shapes=[
                pltpu.VMEM((samples * rows, width), F32),
                pltpu.VMEM((samples * img_rows, width), BF16),
            ],
        ),
        out_shape=[
            jax.ShapeDtypeStruct(text_hidden.shape, BF16),
            jax.ShapeDtypeStruct(img_hidden.shape, BF16),
            jax.ShapeDtypeStruct(latent.shape, F32),
        ],
        compiler_params=pltpu.CompilerParams(vmem_limit_bytes=48 * MIB),
        cost_estimate=pl.CostEstimate(
            flops=2 * samples * rows * width * groups * 4 * head_dim,
            bytes_accessed=4 * groups * 2 * head_dim * width * 2,
            transcendentals=0,
        ),
        name="finish",
    )(col, att, own_w, other_w, text_hidden, img_hidden, mod, w_final, latent)


def per_device(
    img_hidden,
    text_hidden,
    latent,
    text_len,
    block_keep,
    img_pos,
    modulation,
    qk_gain,
    w_qkv,
    w_out,
    w_final,
):
    samples, img_rows, width = img_hidden.shape
    text_rows = text_hidden.shape[1]
    rows = text_rows + img_rows
    head_dim = qk_gain.shape[1]
    groups = w_out.shape[0] // (2 * head_dim)
    tiles = lax.axis_size("row")
    swap = [(0, 1), (1, 0)]
    col = lax.axis_index("col").astype(jnp.int32).reshape(1)
    mod = jnp.transpose(modulation, (1, 0, 2))
    w_heads = jnp.transpose(w_qkv, (1, 0, 2))
    own_w = w_out.reshape(groups, 2, head_dim, width)

    other_pos = lax.ppermute(img_pos, "col", swap)
    normed = norm_tokens(text_hidden, img_hidden, mod)
    other_normed = lax.ppermute(normed, "col", swap)
    other_w = lax.ppermute(own_w, "col", swap)
    rope = jnp.stack(
        [
            jnp.stack(rope_tables(img_pos, text_rows, head_dim)),
            jnp.stack(rope_tables(other_pos, text_rows, head_dim)),
        ]
    )

    mine = lax.axis_index("row") // (tiles // samples)
    used = lax.dynamic_slice(text_len, (mine,), (1,))
    blocks = lax.dynamic_slice(block_keep, (mine, 0), (1, block_keep.shape[1]))
    text_at = jnp.arange(tiles * 2 * text_rows, dtype=jnp.int32).reshape(tiles, 2, text_rows)
    text_bias = jnp.where(text_at < used[0], 0.0, -1e30).astype(F32)
    img_bias = jnp.where(blocks[0][:, None, None] > 0, 0.0, -1e30).astype(F32)
    img_bias = jnp.broadcast_to(img_bias, (tiles, 2, img_rows))
    bias = jnp.concatenate([text_bias, img_bias], axis=2).reshape(1, tiles * 2 * rows)

    attention = None
    gathered = []
    for first, count in ((0, 1), (1, groups - 1)):
        mixed = qkv_heads(col, normed, other_normed, w_heads, rope, qk_gain, first, count)
        mixed = mixed.reshape(tiles, 2 * rows, 3 * count * head_dim)
        packed = lax.all_to_all(mixed, "row", 0, 0, tiled=True)
        gathered.append((first, packed.reshape(tiles * 2 * rows, 3 * count * head_dim)))
    for first, packed in gathered:
        attention = attend(packed, bias, attention, head_dim, 256, first, groups)
    attention = attention.reshape(tiles * 2, rows, groups * head_dim)
    back = lax.all_to_all(attention, ("row", "col"), 0, 0, tiled=True)
    back = back.reshape(samples, 2, 2, rows, groups * head_dim)
    text_out, img_out, latent_next = finish(
        col, back, own_w, other_w, text_hidden, img_hidden, mod, jnp.transpose(w_final), latent,
    )
    return (img_out, text_out, latent_next)


def solution(mesh):
    tokens = P("item", ("row", "col"), None)
    placed = (
        tokens,
        tokens,
        tokens,
        P("item"),
        P("item", None),
        P(("row", "col"), None),
        P("item", None, None),
        P(),
        P(None, None, "col"),
        P("col", None),
        P(),
    )
    return jax.shard_map(
        per_device,
        mesh=mesh,
        in_specs=placed,
        out_specs=(tokens, tokens, tokens),
        check_vma=False,
    )
```

time: 412 us -> 155 us (0.38)
  waiting for transfers between devices: 218 us -> 49.2 us
  local copies, waits for them, and re-layouts: 82.9 us -> 24.7 us
  matrix products: 57.6 us -> 0 us
  Pallas kernels: 0 us -> 56.6 us
  other arithmetic: 33.3 us -> 2.6 us
  starting transfers between devices: 0.65 us -> 20.4 us
  between operations: 14.4 us -> 0.92 us
    all_gather x4 -> x0, waiting for transfers between devices: 195 us -> none  [the longest x1 116 us: per_device(): lax.all_gather(keys, 'row', axis=1, tiled=True)]
    dot_general x5 -> x0, matrix products: 57.6 us -> none  [the longest x1 18.1 us: absorb(): jnp.einsum('shqk,skhd->shqd', weights.astype(jnp.bfloat16), value_split,...]
    pallas_call x0 -> x6, Pallas kernels: none -> 56.6 us  [the longest x2 23.1 us: qkv_heads(): pl.pallas_call(qkv_kernel, grid_spec=pltpu.PrefetchScalarGridSpec(num_sca...]
    all_gather x3 -> x0, local copies, waits for them, and re-layouts: 49.5 us -> none  [the longest x1 24.8 us: per_device(): lax.all_gather(keys, 'row', axis=1, tiled=True)]
    all_to_all x0 -> x3, waiting for transfers between devices: none -> 43.5 us  [the longest x2 24.7 us: per_device(): packed = lax.all_to_all(mixed, 'row', 0, 0, tiled=True)]
    reduce_scatter x2 -> x0, waiting for transfers between devices: 22.5 us -> none  [the longest x1 15.1 us: per_device(): lax.psum_scatter(partial_sum[:, text_rows:].astype(jnp.bfloat16), 'col',...]
    reduce_sum x9 -> x0, other arithmetic: 20 us -> none  [the longest x1 11.8 us: absorb(): total = total * factor + jnp.sum(weights, axis=-1)]
    all_to_all x0 -> x3, starting transfers between devices: none -> 19.7 us  [the longest x2 15.5 us: per_device(): packed = lax.all_to_all(mixed, 'row', 0, 0, tiled=True)]
  transfers between devices with their start and end apart: 6 -> 6, of which waited for: 5 -> 4; matrix products, arithmetic and copies ran while one was open for 22% -> 3% of each run, Pallas kernels for 0% -> 26%
where the time goes in v1:
time: 155 us; the launch traced here: 154 us
  Pallas kernels  56.6 us (37%)
  waiting for transfers between devices  49.2 us (32%)
  local copies, waits for them, and re-layouts  24.7 us (16%)
  starting transfers between devices  20.4 us (13%)
  other arithmetic  2.6 us (2%)
    all_to_all x2, waiting for transfers between devices, per_device(): packed = lax.all_to_all(mixed, 'row', 0, 0, tiled=True)  24.7 us
    unnamed x46, local copies, waits for them, and re-layouts  23.2 us
    pallas_call x2, Pallas kernels, qkv_heads(): pl.pallas_call(qkv_kernel, grid_spec=pltpu.PrefetchScalarGridSpec(num_sca...  23.1 us
    all_to_all x1, waiting for transfers between devices, per_device(): back = lax.all_to_all(attention, ('row', 'col'), 0, 0, tiled=True)  18.8 us
    pallas_call x2, Pallas kernels, attend(): pl.pallas_call(attend_kernel, grid=(count, tokens // block), in_specs=in_...  17 us
    all_to_all x2, starting transfers between devices, per_device(): packed = lax.all_to_all(mixed, 'row', 0, 0, tiled=True)  15.5 us
    pallas_call x1, Pallas kernels, finish(): pl.pallas_call(finish_kernel, grid_spec=pltpu.PrefetchScalarGridSpec(num_...  14 us
    all_to_all x1, starting transfers between devices, per_device(): back = lax.all_to_all(attention, ('row', 'col'), 0, 0, tiled=True)  4.26 us
  transfers between devices with their start and end apart: 6, of which 4 were waited for; matrix products, arithmetic and copies ran while one was open for 3% of the time, Pallas kernels for 26%

profile of v1, /device:TPU:0, one launch (start us, length us, event | category | flops | bytes accessed | tf_op | source)
XLA Modules:
  0.0 154.5 jit_solution(12225458986335306263)
XLA Ops:
  0.6 1.4 copy-done.5
  2.0 1.1 copy-done.8
  3.2 1.0 copy-done.11
  4.2 2.6 %norm_tokens.1.own_ref = bf16[8,48,3072]{2,1,0:T(8,128)(2,1)S(1)} custom-call(bf16[8,16,3072]{2,1,0:T(8,128)(2,1)S(1)} %copy-done.8, bf16[8,32,3072]{2,1,0:T(8,128)(2,1)S(1)} %copy-done.5, f32[5,8,3072]{2,1,0:T(8,128)S(1)} %bitcast.50), custom_call_target="tpu_custom_call" | custom-call | flops 11796480 | bytes 4718592 | tf_op jit(solution)/shard_map/norm_tokens/pallas_call | solution.py:69
  7.5 3.5 %collective-permute-done.1 = s32[32,3]{0,1:T(4,128)S(1)} collective-permute-done((s32[32,3]{0,1:T(4,128)S(1)}, s32[32,3]{0,1:T(4,128)S(1)}, u32[]{:S(2)}, u32[]{:S(2)}) %collective-permute-start.1) | collective-permute-done | bytes 416 | tf_op jit(solution)/shard_map/ppermute | solution.py:319
  11.7 2.2 %collective-permute-done.other_ref = bf16[8,48,3072]{2,1,0:T(8,128)(2,1)} collective-permute-done((bf16[8,48,3072]{2,1,0:T(8,128)(2,1)S(1)}, bf16[8,48,3072]{2,1,0:T(8,128)(2,1)}, u32[]{:S(2)}, u32[]{:S(2)}) %collective-permute-start) | collective-permute-done | bytes 2359328 | tf_op jit(solution)/shard_map/ppermute | solution.py:321
  13.9 5.0 %copy-done = bf16[3072,3,768]{2,0,1:T(8,128)(2,1)S(1)} copy-done((bf16[3072,3,768]{2,0,1:T(8,128)(2,1)S(1)}, bf16[3072,3,768]{2,0,1:T(8,128)(2,1)}, u32[]{:S(2)}) %copy-start) | copy-done | bytes 14155800
  18.9 8.2 %qkv_heads.3 = bf16[8,2,2,48,384]{4,3,2,1,0:T(8,128)(2,1)S(1)} custom-call(s32[1]{0:T(128)} %bitcast.col_ref, bf16[8,48,3072]{2,1,0:T(8,128)(2,1)S(1)} %norm_tokens.1.own_ref, bf16[8,48,3072]{2,1,0:T(8,128)(2,1)} %collective-permute-done.other_ref, bf16[3,3072,768]{2,1,0:T(8,128)(2,1)S(1)} %bitcast.44, f32[2,2,48,128]{3,2,1,0:T(8,128)S(1)} %pad_maximum_fusion.rope_ref, ...), custom_call_target="tpu_custom_call" | custom-call | flops 3623878656 | bytes 9437184 | tf_op jit(solution)/shard_map/qkv_heads/pallas_call | solution.py:126
  27.1 1.0 copy-done.7
  28.1 8.1 %all-to-all-start.1 = ((bf16[16,96,384]{2,1,0:T(8,128)(2,1)}), bf16[16,96,384]{2,1,0:T(8,128)(2,1)S(1)}, u32[]{:S(2)}, u32[]{:S(2)}) async-start(bf16[16,96,384]{2,1,0:T(8,128)(2,1)} %bitcast.47), calls=%async_computation.1 | async-start | bytes 2359296 | tf_op jit(solution)/shard_map/all_to_all | solution.py:344
  36.3 5.0 %copy-done.1 = bf16[3072,3,768]{2,0,1:T(8,128)(2,1)S(1)} copy-done((bf16[3072,3,768]{2,0,1:T(8,128)(2,1)S(1)}, bf16[3072,3,768]{2,0,1:T(8,128)(2,1)}, u32[]{:S(2)}) %copy-start.1) | copy-done | bytes 14155800
  41.3 0.9 copy-done.14
  42.2 14.9 %qkv_heads.2 = bf16[8,2,2,48,768]{4,3,2,1,0:T(8,128)(2,1)S(1)} custom-call(s32[1]{0:T(128)} %bitcast.col_ref, bf16[8,48,3072]{2,1,0:T(8,128)(2,1)S(1)} %norm_tokens.1.own_ref, bf16[8,48,3072]{2,1,0:T(8,128)(2,1)} %collective-permute-done.other_ref, bf16[3,3072,768]{2,1,0:T(8,128)(2,1)S(1)} %bitcast.45, f32[2,2,48,128]{3,2,1,0:T(8,128)S(1)} %copy-done.14, ...), custom_call_target="tpu_custom_call" | custom-call | flops 7247757312 | bytes 14155776 | tf_op jit(solution)/shard_map/qkv_heads/pallas_call | solution.py:126
  57.1 1.4 copy-done.10
  58.6 7.3 %all-to-all-start = ((bf16[16,96,768]{2,1,0:T(8,128)(2,1)}), bf16[16,96,768]{2,1,0:T(8,128)(2,1)S(1)}, u32[]{:S(2)}, u32[]{:S(2)}) async-start(bf16[16,96,768]{2,1,0:T(8,128)(2,1)} %bitcast.49), calls=%async_computation | async-start | bytes 4718592 | tf_op jit(solution)/shard_map/all_to_all | solution.py:344
  65.9 0.6 dynamic_slice.6
  66.5 0.7 fusion.4
  67.2 0.7 compare_select_fusion
  68.0 0.7 pad_maximum_fusion.1
  68.7 0.8 reshape.75.bias_ref
  69.5 5.6 %attend.2.refs_0_ = bf16[1536,384]{1,0:T(8,128)(2,1)S(1)} custom-call(bf16[1536,384]{1,0:T(8,128)(2,1)S(1)} %bitcast.41, bf16[1536,384]{1,0:T(8,128)(2,1)S(1)} %bitcast.42, bf16[1536,384]{1,0:T(8,128)(2,1)S(1)} %bitcast.43, f32[1,1536]{1,0:T(1,128)S(1)} %reshape.75.bias_ref), custom_call_target="tpu_custom_call" | custom-call | flops 1207959552 | bytes 1572864 | tf_op jit(solution)/shard_map/attend/pallas_call | solution.py:181
  75.1 1.0 copy-done.2
  76.1 24.7 %all-to-all-done = bf16[16,96,768]{2,1,0:T(8,128)(2,1)S(1)} async-done(((bf16[16,96,768]{2,1,0:T(8,128)(2,1)}), bf16[16,96,768]{2,1,0:T(8,128)(2,1)S(1)}, u32[]{:S(2)}, u32[]{:S(2)}) %all-to-all-start) | async-done | bytes 2359328 | tf_op jit(solution)/shard_map/all_to_all | solution.py:344
  100.7 1.3 copy-done.3
  102.0 11.4 %attend.3 = bf16[1536,384]{1,0:T(8,128)(2,1)S(1)} custom-call(bf16[1536,768]{1,0:T(8,128)(2,1)S(1)} %bitcast.38, bf16[1536,768]{1,0:T(8,128)(2,1)S(1)} %bitcast.39, bf16[1536,768]{1,0:T(8,128)(2,1)S(1)} %bitcast.40, f32[1,1536]{1,0:T(1,128)S(1)} %reshape.75.bias_ref, bf16[1536,384]{1,0:T(8,128)(2,1)S(1)} %copy-done.3), custom_call_target="tpu_custom_call", output_to_operand_aliasing={{}: (4, {})} | custom-call | flops 2415919104 | bytes 3145728 | tf_op jit(solution)/shard_map/attend/pallas_call | solution.py:181
  113.5 1.0 copy-done.4
  114.5 4.3 %all-to-all-start.2 = ((bf16[32,48,384]{2,1,0:T(8,128)(2,1)}), bf16[32,48,384]{2,1,0:T(8,128)(2,1)S(1)}, u32[]{:S(2)}, u32[]{:S(2)}) async-start(bf16[32,48,384]{2,1,0:T(8,128)(2,1)} %bitcast.46), calls=%async_computation.2 | async-start | bytes 2359296 | tf_op jit(solution)/shard_map/all_to_all | solution.py:349
  118.7 18.8 %all-to-all-done.2 = bf16[32,48,384]{2,1,0:T(8,128)(2,1)S(1)} async-done(((bf16[32,48,384]{2,1,0:T(8,128)(2,1)}), bf16[32,48,384]{2,1,0:T(8,128)(2,1)S(1)}, u32[]{:S(2)}, u32[]{:S(2)}) %all-to-all-start.2) | async-done | bytes 1179680 | tf_op jit(solution)/shard_map/all_to_all | solution.py:349
  137.6 1.0 copy-done.12
  138.6 1.0 copy-done.15
  139.6 0.9 copy-done.16
  140.5 14.0 %finish.1 = (bf16[8,16,3072]{2,1,0:T(8,128)(2,1)}, bf16[8,32,3072]{2,1,0:T(8,128)(2,1)}, f32[8,32,64]{2,1,0:T(8,128)}) custom-call(s32[1]{0:T(128)} %bitcast.col_ref, bf16[8,2,2,48,384]{4,3,2,1,0:T(8,128)(2,1)S(1)} %bitcast.48, bf16[3,2,128,3072]{3,2,1,0:T(8,128)(2,1)} %bitcast.23.own_w_ref, bf16[3,2,128,3072]{3,2,1,0:T(8,128)(2,1)} %collective-permute-done.2.other_w_ref, ...), custom_call_target="tpu_custom_call" | custom-call | flops 3623878656 | bytes 18874368 | tf_op jit(solution)/shard_map/finish/pallas_call | solution.py:258
  (53 shorter events, 1.4 us)
Async XLA Ops:
  0.6 1.4 copy-start.5
  2.0 1.1 copy-start.8
  3.2 1.0 copy-start.11
  4.2 2.7 %copy-start.18 = (s32[32,3]{0,1:T(4,128)S(1)}, s32[32,3]{0,1:T(4,128)}, u32[]{:S(2)}) copy-start(s32[32,3]{0,1:T(4,128)} %param.22) | copy-start | bytes 1156
  4.2 6.8 %copy-start.19 = (f32[64]{0:T(128)S(1)}, f32[64]{0:T(128)}, u32[]{:S(2)}) copy-start(f32[64]{0:T(128)} %constant.45.clone) | copy-start | bytes 772
  4.2 6.8 %copy-start.20 = (f32[64]{0:T(128)S(1)}, f32[64]{0:T(128)}, u32[]{:S(2)}) copy-start(f32[64]{0:T(128)} %constant.44.clone) | copy-start | bytes 772
  4.2 6.9 %copy-start.21 = (f32[64]{0:T(128)S(1)}, f32[64]{0:T(128)}, u32[]{:S(2)}) copy-start(f32[64]{0:T(128)} %constant.43.clone) | copy-start | bytes 772
  4.2 9.6 %copy-start.17 = (f32[2,128]{1,0:T(2,128)S(1)}, f32[2,128]{1,0:T(2,128)}, u32[]{:S(2)}) copy-start(f32[2,128]{1,0:T(2,128)} %gain_ref.3) | copy-start | bytes 3076
  6.8 7.1 %collective-permute-start = (bf16[8,48,3072]{2,1,0:T(8,128)(2,1)S(1)}, bf16[8,48,3072]{2,1,0:T(8,128)(2,1)}, u32[]{:S(2)}, u32[]{:S(2)}) collective-permute-start(bf16[8,48,3072]{2,1,0:T(8,128)(2,1)S(1)} %norm_tokens.1.own_ref), channel_id=1, source_target_pairs={{0,1},{1,0},{2,3},{3,2},{4,5},{5,4},{6,7},{7,6},{8,9},{9,8},{10,11... | collective-permute-start | bytes 7077896 | tf_op jit(solution)/shard_map/ppermute | solution.py:321
  6.9 4.1 %collective-permute-start.1 = (s32[32,3]{0,1:T(4,128)S(1)}, s32[32,3]{0,1:T(4,128)S(1)}, u32[]{:S(2)}, u32[]{:S(2)}) collective-permute-start(s32[32,3]{0,1:T(4,128)S(1)} %copy-done.18), channel_id=1, source_target_pairs={{0,1},{1,0},{2,3},{3,2},{4,5},{5,4},{6,7},{7,6},{8,9},{9,8},{10,11... | collective-permute-start | bytes 1160 | tf_op jit(solution)/shard_map/ppermute | solution.py:319
  7.4 111.3 %collective-permute-start.2 = (bf16[3,2,128,3072]{3,2,1,0:T(8,128)(2,1)}, bf16[3,2,128,3072]{3,2,1,0:T(8,128)(2,1)}, u32[]{:S(2)}, u32[]{:S(2)}) collective-permute-start(bf16[3,2,128,3072]{3,2,1,0:T(8,128)(2,1)} %bitcast.23.own_w_ref), channel_id=1, source_target_pairs={{0,1},{1,0},{2,3},{3,2},{4,5},{5,4},{6,7},{7,6},{8,9},{9,8},{10,11... | collective-permute-start | bytes 14155784 | tf_op jit(solution)/shard_map/ppermute | solution.py:322
  11.7 15.4 %copy-start.13 = (f32[2,2,48,128]{3,2,1,0:T(8,128)}, f32[2,2,48,128]{3,2,1,0:T(8,128)S(1)}, u32[]{:S(2)}) copy-start(f32[2,2,48,128]{3,2,1,0:T(8,128)S(1)} %pad_maximum_fusion.rope_ref) | copy-start | bytes 294916
  13.9 5.0 %copy-start = (bf16[3072,3,768]{2,0,1:T(8,128)(2,1)S(1)}, bf16[3072,3,768]{2,0,1:T(8,128)(2,1)}, u32[]{:S(2)}) copy-start(bf16[3072,3,768]{2,0,1:T(8,128)(2,1)} %param.25) | copy-start | bytes 42467332
  27.1 1.0 copy-start.7
  28.1 30.4 %all-to-all-start.1 = ((bf16[16,96,384]{2,1,0:T(8,128)(2,1)}), bf16[16,96,384]{2,1,0:T(8,128)(2,1)S(1)}, u32[]{:S(2)}, u32[]{:S(2)}) async-start(bf16[16,96,384]{2,1,0:T(8,128)(2,1)} %bitcast.47), calls=%async_computation.1 | async-start | bytes 2359296 | tf_op jit(solution)/shard_map/all_to_all | solution.py:344
  36.3 5.0 %copy-start.1 = (bf16[3072,3,768]{2,0,1:T(8,128)(2,1)S(1)}, bf16[3072,3,768]{2,0,1:T(8,128)(2,1)}, u32[]{:S(2)}) copy-start(bf16[3072,3,768]{2,0,1:T(8,128)(2,1)} %param.25) | copy-start | bytes 42467332
  41.3 0.9 copy-start.14
  57.1 1.4 copy-start.10
  58.6 7.4 %copy-start.22 = (s32[8]{0:T(128)S(1)}, s32[8]{0:T(128)}, u32[]{:S(2)}) copy-start(s32[8]{0:T(128)} %param.20) | copy-start | bytes 100
  58.6 42.2 %all-to-all-start = ((bf16[16,96,768]{2,1,0:T(8,128)(2,1)}), bf16[16,96,768]{2,1,0:T(8,128)(2,1)S(1)}, u32[]{:S(2)}, u32[]{:S(2)}) async-start(bf16[16,96,768]{2,1,0:T(8,128)(2,1)} %bitcast.49), calls=%async_computation | async-start | bytes 4718592 | tf_op jit(solution)/shard_map/all_to_all | solution.py:344
  75.1 1.0 copy-start.2
  100.7 1.3 copy-start.3
  113.4 1.0 copy-start.4
  114.5 23.1 %copy-start.6 = (bf16[8,32,3072]{2,1,0:T(8,128)(2,1)S(1)}, bf16[8,32,3072]{2,1,0:T(8,128)(2,1)}, u32[]{:S(2)}) copy-start(bf16[8,32,3072]{2,1,0:T(8,128)(2,1)} %img_ref.3) | copy-start | bytes 4718596
  114.5 23.1 %copy-start.9 = (bf16[8,16,3072]{2,1,0:T(8,128)(2,1)S(1)}, bf16[8,16,3072]{2,1,0:T(8,128)(2,1)}, u32[]{:S(2)}) copy-start(bf16[8,16,3072]{2,1,0:T(8,128)(2,1)} %text_ref.3) | copy-start | bytes 2359300
  114.5 23.1 %all-to-all-start.2 = ((bf16[32,48,384]{2,1,0:T(8,128)(2,1)}), bf16[32,48,384]{2,1,0:T(8,128)(2,1)S(1)}, u32[]{:S(2)}, u32[]{:S(2)}) async-start(bf16[32,48,384]{2,1,0:T(8,128)(2,1)} %bitcast.46), calls=%async_computation.2 | async-start | bytes 2359296 | tf_op jit(solution)/shard_map/all_to_all | solution.py:349
  137.6 1.0 copy-start.12
  138.6 1.0 copy-start.15
  139.6 0.9 copy-start.16

commit v2 on v1

v2 whole, which is shorter than its diff:
```python
import functools
import math

import jax
import jax.numpy as jnp
import numpy as np
from jax import lax
from jax.experimental import pallas as pl
from jax.experimental.pallas import tpu as pltpu
from jax.sharding import PartitionSpec as P

eps_norm = 1e-06
theta_base = 10000.0
step_size = -0.25
excluded = -1e30
MIB = 1 << 20
F32 = jnp.float32
BF16 = jnp.bfloat16


def in_hbm(array):
    return pltpu.with_memory_space_constraint(array, pltpu.HBM)


def in_vmem():
    return pl.BlockSpec(memory_space=pltpu.VMEM)


def in_place():
    return pl.BlockSpec(memory_space=pl.ANY)


def rope_rates(head_dim):
    half = head_dim // 2
    first = head_dim // 16
    second = (half - first) // 2
    counts = [first, second, half - first - second]
    tables = []
    for axis_id in range(3):
        pieces = []
        for other in range(3):
            if other == axis_id:
                pieces.append(theta_base ** (-np.arange(counts[other]) / counts[other]))
            else:
                pieces.append(np.zeros(counts[other]))
        tables.append(np.concatenate(pieces + pieces).astype(np.float32))
    return np.stack(tables)


def layer_norm(values):
    center = values - jnp.mean(values, axis=-1, keepdims=True)
    return center * lax.rsqrt(jnp.mean(center * center, axis=-1, keepdims=True) + eps_norm)


def norm_kernel(text_ref, img_ref, mod_ref, out_ref):
    s = pl.program_id(0)
    text_rows = text_ref.shape[1]
    shift = mod_ref[0, pl.ds(s, 1), :]
    scale = 1.0 + mod_ref[1, pl.ds(s, 1), :]
    out_ref[0, :text_rows] = (scale * layer_norm(text_ref[0].astype(F32)) + shift).astype(BF16)
    out_ref[0, text_rows:] = (scale * layer_norm(img_ref[0].astype(F32)) + shift).astype(BF16)


def norm_tokens(text_hidden, img_hidden, mod):
    samples, text_rows, width = text_hidden.shape
    img_rows = img_hidden.shape[1]
    rows = text_rows + img_rows
    return pl.pallas_call(
        norm_kernel,
        grid=(samples,),
        in_specs=[
            pl.BlockSpec((1, text_rows, width), lambda s: (s, 0, 0)),
            pl.BlockSpec((1, img_rows, width), lambda s: (s, 0, 0)),
            pl.BlockSpec((2, samples, width), lambda s: (0, 0, 0)),
        ],
        out_specs=pl.BlockSpec((1, rows, width), lambda s: (s, 0, 0)),
        out_shape=jax.ShapeDtypeStruct((samples, rows, width), BF16),
        compiler_params=pltpu.CompilerParams(vmem_limit_bytes=16 * MIB),
        cost_estimate=pl.CostEstimate(
            flops=samples * rows * width * 10,
            bytes_accessed=samples * rows * width * 4,
            transcendentals=0,
        ),
        name="norm_tokens",
    )(in_hbm(text_hidden), in_hbm(img_hidden), in_hbm(mod))


def qkv_kernel(*refs, halves, first, count):
    x_refs, pos_refs = refs[: len(halves)], refs[len(halves) : 2 * len(halves)]
    w_hbm, rates_ref, gain_ref = refs[2 * len(halves) : 2 * len(halves) + 3]
    out_hbm, w_buf, stage, w_sems, out_sems = refs[-5:]
    samples, rows, width = x_refs[0].shape
    head_dim = gain_ref.shape[1]
    img_rows = pos_refs[0].shape[1]
    col = lax.axis_index("col")
    steps = [(j, t) for j in range(count) for t in range(3)]
    loads = []
    for n, (j, t) in enumerate(steps):
        columns = pl.ds((first + j) * 2 * head_dim, 2 * head_dim)
        loads.append(pltpu.make_async_copy(w_hbm.at[t, :, columns], w_buf.at[n], w_sems.at[n]))
        loads[-1].start()
    turns = []
    for pos_ref in pos_refs:
        angle = lax.dot_general(
            pos_ref[...].astype(F32), rates_ref[...], (((0,), (0,)), ((), ())),
            precision=lax.Precision.HIGHEST, preferred_element_type=F32,
        )
        angle = jnp.concatenate([jnp.zeros((rows - img_rows, head_dim), F32), angle], axis=0)
        lane = lax.broadcasted_iota(jnp.int32, angle.shape, 1)
        sine = jnp.sin(angle)
        turns.append((jnp.cos(angle), jnp.where(lane < head_dim // 2, -sine, sine)))
    stores = []
    for n, (j, t) in enumerate(steps):
        loads[n].wait()
        for h, x_ref in enumerate(x_refs):
            slot = n * len(halves) + h
            y = jnp.dot(
                x_ref[...].reshape(samples * rows, width), w_buf[n], preferred_element_type=F32
            )
            for hh in range(2):
                v = y[:, hh * head_dim : (hh + 1) * head_dim]
                if t < 2:
                    v = v * lax.rsqrt(jnp.mean(v * v, axis=-1, keepdims=True) + eps_norm)
                    v = v * gain_ref[t : t + 1, :]
                    rolled = pltpu.roll(v, head_dim // 2, 1).reshape(samples, rows, head_dim)
                    cosine, sine = turns[h]
                    v = v.reshape(samples, rows, head_dim) * cosine[None] + rolled * sine[None]
                stage[slot, :, hh] = v.reshape(samples, rows, head_dim).astype(BF16)
            place = col if halves[h] == 0 else 1 - col
            stores.append(
                pltpu.make_async_copy(
                    stage.at[slot], out_hbm.at[:, :, 3 * j + t, place], out_sems.at[slot]
                )
            )
            stores[-1].start()
    for store in stores:
        store.wait()


def qkv_heads(xs, positions, halves, w_qkv, gain, before, first, count):
    samples, rows, width = xs[0].shape
    head_dim = gain.shape[1]
    operands = [*xs, *positions, in_hbm(w_qkv), rope_rates(head_dim), gain]
    in_specs = [in_vmem() for _ in operands]
    in_specs[2 * len(xs)] = in_place()
    if before is not None:
        operands.append(in_hbm(before))
        in_specs.append(in_place())
    steps = 3 * count
    return pl.pallas_call(
        functools.partial(qkv_kernel, halves=halves, first=first, count=count),
        in_specs=in_specs,
        out_specs=in_place(),
        out_shape=pltpu.HBM((samples, 2, steps, 2, rows, head_dim), BF16),
        input_output_aliases={} if before is None else {len(operands) - 1: 0},
        scratch_shapes=[
            pltpu.VMEM((steps, width, 2 * head_dim), BF16),
            pltpu.VMEM((steps * len(xs), samples, 2, rows, head_dim), BF16),
            pltpu.SemaphoreType.DMA((steps,)),
            pltpu.SemaphoreType.DMA((steps * len(xs),)),
        ],
        compiler_params=pltpu.CompilerParams(vmem_limit_bytes=40 * MIB),
        cost_estimate=pl.CostEstimate(
            flops=2 * samples * len(xs) * rows * width * 2 * steps * head_dim,
            bytes_accessed=2 * (len(xs) * samples * rows * width + width * 2 * steps * head_dim),
            transcendentals=0,
        ),
        name="qkv_heads",
    )(*operands)


def attend_kernel(used_ref, keep_ref, q_ref, k_ref, v_ref, *refs, samples, text_rows, block):
    out_ref, wide_k, wide_v = refs[-3:]
    tiles, tile, head_dim = q_ref.shape
    tokens = tiles * tile
    rows = out_ref.shape[2]
    factor = math.log2(math.e) / math.sqrt(head_dim)

    @pl.when(pl.program_id(0) == 0)
    def _():
        mine = lax.axis_index("row") // (tiles // samples)
        used = used_ref[mine]
        at = lax.broadcasted_iota(jnp.int32, (tile, head_dim), 0)
        inner = at % rows
        text_at = (at // rows) * text_rows + inner
        for r in range(tiles):
            text_bias = jnp.where(text_at + r * 2 * text_rows < used, 0.0, excluded)
            img_bias = jnp.where(keep_ref[mine, r] > 0, 0.0, excluded)
            bias = jnp.where(inner < text_rows, text_bias, img_bias)
            wide_k[r * tile : (r + 1) * tile, head_dim:] = bias.astype(BF16)
        wide_v[:, head_dim:] = jnp.ones((tokens, head_dim), BF16)

    wide_k[:, :head_dim] = k_ref[...].reshape(tokens, head_dim)
    wide_v[:, :head_dim] = v_ref[...].reshape(tokens, head_dim)
    lane = lax.broadcasted_iota(jnp.int32, (block, head_dim), 1)
    one = jnp.where(lane == 0, 1.0, 0.0).astype(BF16)
    q = q_ref[...].reshape(tokens, head_dim)
    for m in range(0, tokens, block):
        wide_q = jnp.concatenate([q[m : m + block], one], axis=1)
        scores = lax.dot_general(
            wide_q, wide_k[...], (((1,), (1,)), ((), ())), preferred_element_type=F32
        )
        top = jnp.max(scores, axis=-1, keepdims=True)
        weights = jnp.exp2((scores - top) * factor).astype(BF16)
        summed = jnp.dot(weights, wide_v[...], preferred_element_type=F32)
        result = (summed[:, :head_dim] / summed[:, head_dim:]).astype(BF16)
        per = block // rows
        place = m // rows
        result = result.reshape(per, rows, head_dim)
        for p in range(per):
            out_ref[(place + p) // 2, (place + p) % 2] = result[p]


def attend(packed, text_len, block_keep, before, rows, text_rows, block, first, heads):
    tiles, steps, tile, head_dim = packed.shape
    count = steps // 3
    tokens = tiles * tile
    samples = text_len.shape[0]
    part = lambda t: pl.BlockSpec((tiles, None, tile, head_dim), lambda j: (0, 3 * j + t, 0, 0))
    smem = pl.BlockSpec(memory_space=pltpu.SMEM)
    operands = [text_len, block_keep, packed, packed, packed]
    in_specs = [smem, smem, part(0), part(1), part(2)]
    if before is not None:
        operands.append(in_hbm(before))
        in_specs.append(in_place())
    return pl.pallas_call(
        functools.partial(
            attend_kernel, samples=samples, text_rows=text_rows, block=block
        ),
        grid=(count,),
        in_specs=in_specs,
        out_specs=pl.BlockSpec(
            (tiles, 2, None, rows, head_dim), lambda j: (0, 0, first + j, 0, 0)
        ),
        out_shape=pltpu.HBM((tiles, 2, heads, rows, head_dim), BF16),
        input_output_aliases={} if before is None else {5: 0},
        scratch_shapes=[
            pltpu.VMEM((tokens, 2 * head_dim), BF16),
            pltpu.VMEM((tokens, 2 * head_dim), BF16),
        ],
        compiler_params=pltpu.CompilerParams(vmem_limit_bytes=40 * MIB),
        cost_estimate=pl.CostEstimate(
            flops=8 * count * tokens * tokens * head_dim,
            bytes_accessed=2 * 4 * count * tokens * head_dim,
            transcendentals=count * tokens * tokens,
        ),
        name="attend",
    )(*operands)


def finish_kernel(
    att_ref, own_w, other_w, text_hbm, img_hbm, mod_hbm, wf_hbm, latent_hbm,
    text_out_ref, img_out_ref, next_ref,
    w_buf, text, img, mod, wf, latent, acc, final, sems,
):
    samples, _, _, heads, rows, head_dim = att_ref.shape
    width = own_w.shape[-1]
    text_rows, img_rows = text.shape[1], img.shape[1]
    col = lax.axis_index("col")
    loads = []
    for hh in range(2):
        for k, (source, place) in enumerate(((own_w, col), (other_w, 1 - col))):
            loads.append(
                pltpu.make_async_copy(
                    source.at[:, hh], w_buf.at[hh, place], sems.at[2 * hh + k]
                )
            )
    others = [
        pltpu.make_async_copy(source, buf, sems.at[4 + k])
        for k, (source, buf) in enumerate(
            ((text_hbm, text), (img_hbm, img), (mod_hbm, mod), (wf_hbm, wf), (latent_hbm, latent))
        )
    ]
    for copy in loads + others:
        copy.start()

    def lhs(hh, low, high):
        pieces = [
            att_ref[low:high, hh, c, j].reshape((high - low) * rows, head_dim)
            for c in range(2)
            for j in range(heads)
        ]
        return jnp.concatenate(pieces, axis=1)

    def weight(hh):
        return w_buf[hh].reshape(2 * heads * head_dim, width)

    loads[0].wait()
    loads[1].wait()
    acc[...] = jnp.dot(lhs(0, 0, samples), weight(0), preferred_element_type=F32)
    loads[2].wait()
    loads[3].wait()
    for copy in others:
        copy.wait()
    group = samples // 2
    for low in range(0, samples, group):
        sums = acc[low * rows : (low + group) * rows]
        acc[low * rows : (low + group) * rows] = sums + jnp.dot(
            lhs(1, low, low + group), weight(1), preferred_element_type=F32
        )
        for s in range(low, low + group):
            gate = mod[2, s : s + 1, :]
            text_sum = acc[s * rows : s * rows + text_rows]
            text_out_ref[s] = (text[s].astype(F32) + gate * text_sum).astype(BF16)
            img_sum = acc[s * rows + text_rows : (s + 1) * rows]
            new_img = (img[s].astype(F32) + gate * img_sum).astype(BF16)
            img_out_ref[s] = new_img
            scaled = (1.0 + mod[4, s : s + 1, :]) * layer_norm(new_img.astype(F32))
            final[s * img_rows : (s + 1) * img_rows] = (scaled + mod[3, s : s + 1, :]).astype(BF16)
    velocity = lax.dot_general(
        final[...], wf[...], (((1,), (1,)), ((), ())), preferred_element_type=F32
    )
    next_ref[...] = latent[...] + step_size * velocity.reshape(latent.shape)


def finish(att, own_w, other_w, text_hidden, img_hidden, mod, w_final, latent):
    samples, text_rows, width = text_hidden.shape
    img_rows = img_hidden.shape[1]
    rows = text_rows + img_rows
    groups, _, head_dim, _ = own_w.shape
    return pl.pallas_call(
        finish_kernel,
        in_specs=[in_vmem()] + [in_place()] * 7,
        out_specs=[in_vmem()] * 3,
        out_shape=[
            pltpu.HBM(text_hidden.shape, BF16),
            pltpu.HBM(img_hidden.shape, BF16),
            pltpu.HBM(latent.shape, F32),
        ],
        scratch_shapes=[
            pltpu.VMEM((2, 2, groups, head_dim, width), BF16),
            pltpu.VMEM(text_hidden.shape, BF16),
            pltpu.VMEM(img_hidden.shape, BF16),
            pltpu.VMEM(mod.shape, F32),
            pltpu.VMEM(w_final.shape, BF16),
            pltpu.VMEM(latent.shape, F32),
            pltpu.VMEM((samples * rows, width), F32),
            pltpu.VMEM((samples * img_rows, width), BF16),
            pltpu.SemaphoreType.DMA((9,)),
        ],
        compiler_params=pltpu.CompilerParams(vmem_limit_bytes=48 * MIB),
        cost_estimate=pl.CostEstimate(
            flops=2 * samples * rows * width * groups * 4 * head_dim,
            bytes_accessed=4 * groups * 2 * head_dim * width * 2,
            transcendentals=0,
        ),
        name="finish",
    )(
        att, in_hbm(own_w), in_hbm(other_w), in_hbm(text_hidden), in_hbm(img_hidden),
        in_hbm(mod), in_hbm(w_final), in_hbm(latent),
    )


def per_device(
    img_hidden,
    text_hidden,
    latent,
    text_len,
    block_keep,
    img_pos,
    modulation,
    qk_gain,
    w_qkv,
    w_out,
    w_final,
):
    samples, img_rows, width = img_hidden.shape
    text_rows = text_hidden.shape[1]
    rows = text_rows + img_rows
    head_dim = qk_gain.shape[1]
    groups = w_out.shape[0] // (2 * head_dim)
    tiles = lax.axis_size("row")
    swap = [(0, 1), (1, 0)]
    mod = jnp.transpose(modulation, (1, 0, 2))
    w_heads = jnp.transpose(w_qkv, (1, 0, 2))
    own_w = w_out.reshape(groups, 2, head_dim, width)
    pos = jnp.transpose(img_pos)

    normed = norm_tokens(text_hidden, img_hidden, mod)
    other_normed = lax.ppermute(normed, "col", swap)
    other_pos = lax.ppermute(pos, "col", swap)
    other_w = lax.ppermute(own_w, "col", swap)

    def exchange(mixed):
        mixed = mixed.reshape(tiles, mixed.shape[2], 2 * rows, head_dim)
        return lax.all_to_all(mixed, "row", 0, 0, tiled=True)

    mixed = qkv_heads([normed], [pos], (0,), w_heads, qk_gain, None, 0, 1)
    mixed = qkv_heads([other_normed], [other_pos], (1,), w_heads, qk_gain, mixed, 0, 1)
    packed = exchange(mixed)
    late = qkv_heads(
        [normed, other_normed], [pos, other_pos], (0, 1), w_heads, qk_gain, None, 1, groups - 1
    )
    late = exchange(late)
    attention = attend(packed, text_len, block_keep, None, rows, text_rows, 384, 0, groups)
    attention = attend(late, text_len, block_keep, attention, rows, text_rows, 384, 1, groups)
    attention = attention.reshape(tiles * 2, groups, rows, head_dim)
    back = lax.all_to_all(attention, ("row", "col"), 0, 0, tiled=True)
    back = back.reshape(samples, 2, 2, groups, rows, head_dim)
    text_out, img_out, latent_next = finish(
        back, own_w, other_w, text_hidden, img_hidden, mod, jnp.transpose(w_final), latent
    )
    return (img_out, text_out, latent_next)


def solution(mesh):
    tokens = P("item", ("row", "col"), None)
    placed = (
        tokens,
        tokens,
        tokens,
        P("item"),
        P("item", None),
        P(("row", "col"), None),
        P("item", None, None),
        P(),
        P(None, None, "col"),
        P("col", None),
        P(),
    )
    return jax.shard_map(
        per_device,
        mesh=mesh,
        in_specs=placed,
        out_specs=(tokens, tokens, tokens),
        check_vma=False,
    )
```

time: 155 us -> 128 us (0.83)
  local copies, waits for them, and re-layouts: 24.7 us -> 1.69 us
  waiting for transfers between devices: 49.2 us -> 52.5 us
  starting transfers between devices: 20.4 us -> 17.3 us
  other arithmetic: 2.6 us -> 0 us
    unnamed x46 -> x14, local copies, waits for them, and re-layouts: 23.2 us -> 1.69 us
    all_to_all x2, waiting for transfers between devices: 24.7 us -> 33.7 us  [exchange(): return lax.all_to_all(mixed, 'row', 0, 0, tiled=True)]
    pallas_call x5 -> x6, Pallas kernels: 54.1 us -> 49.7 us  [the longest x3 26.9 us: qkv_heads(): pl.pallas_call(functools.partial(qkv_kernel, halves=halves, first=first,...]
    ppermute x1, waiting for transfers between devices: 3.55 us -> 0.01 us  [per_device(): other_pos = lax.ppermute(pos, 'col', swap)]
    all_to_all x2, starting transfers between devices: 15.5 us -> 12.2 us  [exchange(): return lax.all_to_all(mixed, 'row', 0, 0, tiled=True)]
    pallas_call x1, Pallas kernels: 2.55 us -> 5.72 us  [norm_tokens(): pl.pallas_call(norm_kernel, grid=(samples,), in_specs=[pl.BlockSpec((1, t...]
    ppermute x1, waiting for transfers between devices: 2.17 us -> 0.01 us  [per_device(): other_normed = lax.ppermute(normed, 'col', swap)]
  transfers between devices with their start and end apart: 6 -> 6, of which waited for: 4 -> 3; matrix products, arithmetic and copies ran while one was open for 3% -> 0% of each run, Pallas kernels for 26% -> 26%
where the time goes in v2:
time: 128 us
  Pallas kernels  55.4 us (43%)
  waiting for transfers between devices  52.5 us (41%)
  starting transfers between devices  17.3 us (14%)
  local copies, waits for them, and re-layouts  1.69 us (1%)
    all_to_all x2, waiting for transfers between devices, exchange(): return lax.all_to_all(mixed, 'row', 0, 0, tiled=True)  33.7 us
    pallas_call x3, Pallas kernels, qkv_heads(): pl.pallas_call(functools.partial(qkv_kernel, halves=halves, first=first,...  26.9 us
    all_to_all x1, waiting for transfers between devices, per_device(): back = lax.all_to_all(attention, ('row', 'col'), 0, 0, tiled=True)  18.7 us
    pallas_call x2, Pallas kernels, attend(): pl.pallas_call(functools.partial(attend_kernel, samples=samples, text_row...  13.8 us
    all_to_all x2, starting transfers between devices, exchange(): return lax.all_to_all(mixed, 'row', 0, 0, tiled=True)  12.2 us
    pallas_call x1, Pallas kernels, finish(): pl.pallas_call(finish_kernel, in_specs=[in_vmem()] + [in_place()] * 7, ou...  8.92 us
    pallas_call x1, Pallas kernels, norm_tokens(): pl.pallas_call(norm_kernel, grid=(samples,), in_specs=[pl.BlockSpec((1, t...  5.72 us
    all_to_all x1, starting transfers between devices, per_device(): back = lax.all_to_all(attention, ('row', 'col'), 0, 0, tiled=True)  4.2 us
  transfers between devices with their start and end apart: 6, of which 3 were waited for; matrix products, arithmetic and copies ran while one was open for 0% of the time, Pallas kernels for 26%

profile of v2, /device:TPU:0, one launch (start us, length us, event | category | flops | bytes accessed | tf_op | source)
XLA Modules:
  0.0 127.9 jit_solution(13568985043603126231)
XLA Ops:
  0.6 0.0 copy-start.4
  0.6 0.0 copy-start.2
  0.7 0.0 copy-start.3
  0.7 5.7 %norm_tokens.1.refs_0_ = bf16[8,48,3072]{2,1,0:T(8,128)(2,1)S(1)} custom-call(bf16[8,16,3072]{2,1,0:T(8,128)(2,1)} %text_hbm.1, bf16[8,32,3072]{2,1,0:T(8,128)(2,1)} %img_hbm.1, f32[5,8,3072]{2,1,0:T(8,128)} %bitcast.20), custom_call_target="tpu_custom_call" | custom-call | flops 11796480 | bytes 4718592 | tf_op jit(solution)/shard_map/norm_tokens/pallas_call | solution.py:68
  6.4 0.1 collective-permute-start
  6.5 0.0 copy-done.4
  6.5 0.5 collective-permute-start.1
  7.0 0.0 copy-done.2
  7.0 0.0 copy-done.3
  7.0 6.4 %qkv_heads.4.refs_5_ = bf16[8,2,3,2,48,128]{5,4,3,2,1,0:T(8,128)(2,1)} custom-call(bf16[8,48,3072]{2,1,0:T(8,128)(2,1)S(1)} %norm_tokens.1.refs_0_, s32[3,32]{1,0:T(4,128)S(1)} %bitcast.11, bf16[3,3072,768]{2,1,0:T(8,128)(2,1)} %bitcast.13, f32[3,128]{1,0:T(4,128)S(1)} %copy-done.2, f32[2,128]{1,0:T(2,128)S(1)} %copy-done.3), custom_call_target="tpu_custom_call" | custom-call | flops 1811939328 | bytes 7077888 | tf_op jit(solution)/shard_map/qkv_heads/pallas_call | solution.py:150
  13.4 0.0 collective-permute-done.1.refs_3_.refs_1_
  13.4 0.0 collective-permute-done.refs_1_.refs_0_
  13.4 0.0 copy-start
  13.4 7.2 %qkv_heads.5 = bf16[8,2,3,2,48,128]{5,4,3,2,1,0:T(8,128)(2,1)} custom-call(bf16[8,48,3072]{2,1,0:T(8,128)(2,1)S(1)} %collective-permute-done.refs_1_.refs_0_, s32[3,32]{1,0:T(4,128)S(1)} %collective-permute-done.1.refs_3_.refs_1_, bf16[3,3072,768]{2,1,0:T(8,128)(2,1)} %bitcast.14, f32[3,128]{1,0:T(4,128)S(1)} %copy-done.2, ...), custom_call_target="tpu_custom_call", output_to_operand_aliasing={{}: (5, {})} | custom-call | flops 1811939328 | bytes 7077888 | tf_op jit(solution)/shard_map/qkv_heads/pallas_call | solution.py:150
  20.6 0.0 copy-done
  20.6 8.1 %all-to-all-start.1 = ((bf16[16,3,96,128]{3,2,1,0:T(8,128)(2,1)}), bf16[16,3,96,128]{3,2,1,0:T(8,128)(2,1)S(1)}, u32[]{:S(2)}, u32[]{:S(2)}) async-start(bf16[16,3,96,128]{3,2,1,0:T(8,128)(2,1)} %bitcast.16), calls=%async_computation.1 | async-start | bytes 2359296 | tf_op jit(solution)/shard_map/all_to_all | solution.py:386
  28.8 0.3 collective-permute-start.2
  29.1 0.0 copy-start.1
  29.1 1.7 %copy-done.1 = bf16[8,48,3072]{2,1,0:T(8,128)(2,1)S(1)} copy-done((bf16[8,48,3072]{2,1,0:T(8,128)(2,1)S(1)}, bf16[8,48,3072]{2,1,0:T(8,128)(2,1)}, u32[]{:S(2)}) %copy-start.1) | copy-done | bytes 2359320
  30.7 13.4 %qkv_heads.3 = bf16[8,2,6,2,48,128]{5,4,3,2,1,0:T(8,128)(2,1)} custom-call(bf16[8,48,3072]{2,1,0:T(8,128)(2,1)S(1)} %norm_tokens.1.refs_0_, bf16[8,48,3072]{2,1,0:T(8,128)(2,1)S(1)} %copy-done.1, s32[3,32]{1,0:T(4,128)S(1)} %bitcast.12, s32[3,32]{1,0:T(4,128)S(1)} %collective-permute-done.1.refs_3_.refs_1_, bf16[3,3072,768]{2,1,0:T(8,128)(2,1)} %bitcast.15, ...), custom_call_target="tpu_custom_call" | custom-call | flops 7247757312 | bytes 14155776 | tf_op jit(solution)/shard_map/qkv_heads/pallas_call | solution.py:150
  44.1 4.3 %all-to-all-done.1.q_ref.k_ref.v_ref = bf16[16,3,96,128]{3,2,1,0:T(8,128)(2,1)S(1)} async-done(((bf16[16,3,96,128]{3,2,1,0:T(8,128)(2,1)}), bf16[16,3,96,128]{3,2,1,0:T(8,128)(2,1)S(1)}, u32[]{:S(2)}, u32[]{:S(2)}) %all-to-all-start.1) | async-done | bytes 1179680 | tf_op jit(solution)/shard_map/all_to_all | solution.py:386
  48.3 0.0 copy-start.6
  48.4 4.1 %all-to-all-start = ((bf16[16,6,96,128]{3,2,1,0:T(8,128)(2,1)}), bf16[16,6,96,128]{3,2,1,0:T(8,128)(2,1)S(1)}, u32[]{:S(2)}, u32[]{:S(2)}) async-start(bf16[16,6,96,128]{3,2,1,0:T(8,128)(2,1)} %bitcast.19), calls=%async_computation | async-start | bytes 4718592 | tf_op jit(solution)/shard_map/all_to_all | solution.py:386
  52.4 0.0 copy-done.5
  52.4 0.0 copy-done.6
  52.5 5.0 %attend.2.refs_0_ = bf16[16,2,3,48,128]{4,3,2,1,0:T(8,128)(2,1)} custom-call(s32[8]{0:T(128)S(1)} %copy-done.6, s32[8,16]{1,0:T(8,128)S(1)} %copy-done.5, bf16[16,3,96,128]{3,2,1,0:T(8,128)(2,1)S(1)} %all-to-all-done.1.q_ref.k_ref.v_ref, bf16[16,3,96,128]{3,2,1,0:T(8,128)(2,1)S(1)} %all-to-all-done.1.q_ref.k_ref.v_ref, ...), custom_call_target="tpu_custom_call" | custom-call | flops 2415919104 | bytes 1572864 | tf_op jit(solution)/shard_map/attend/pallas_call | solution.py:226
  57.4 29.5 %all-to-all-done.q_ref.k_ref.v_ref = bf16[16,6,96,128]{3,2,1,0:T(8,128)(2,1)S(1)} async-done(((bf16[16,6,96,128]{3,2,1,0:T(8,128)(2,1)}), bf16[16,6,96,128]{3,2,1,0:T(8,128)(2,1)S(1)}, u32[]{:S(2)}, u32[]{:S(2)}) %all-to-all-start) | async-done | bytes 2359328 | tf_op jit(solution)/shard_map/all_to_all | solution.py:386
  86.9 8.8 %attend.3 = bf16[16,2,3,48,128]{4,3,2,1,0:T(8,128)(2,1)} custom-call(s32[8]{0:T(128)S(1)} %copy-done.6, s32[8,16]{1,0:T(8,128)S(1)} %copy-done.5, bf16[16,6,96,128]{3,2,1,0:T(8,128)(2,1)S(1)} %all-to-all-done.q_ref.k_ref.v_ref, bf16[16,6,96,128]{3,2,1,0:T(8,128)(2,1)S(1)} %all-to-all-done.q_ref.k_ref.v_ref, ...), custom_call_target="tpu_custom_call", output_to_operand_aliasing={{}: (5, {})} | custom-call | flops 4831838208 | bytes 3145728 | tf_op jit(solution)/shard_map/attend/pallas_call | solution.py:226
  95.8 4.2 %all-to-all-start.2 = ((bf16[32,3,48,128]{3,2,1,0:T(8,128)(2,1)}), bf16[32,3,48,128]{3,2,1,0:T(8,128)(2,1)S(1)}, u32[]{:S(2)}, u32[]{:S(2)}) async-start(bf16[32,3,48,128]{3,2,1,0:T(8,128)(2,1)} %bitcast.22), calls=%async_computation.2 | async-start | bytes 2359296 | tf_op jit(solution)/shard_map/all_to_all | solution.py:398
  100.0 0.0 collective-permute-done.2.other_w
  100.0 18.7 %all-to-all-done.2 = bf16[32,3,48,128]{3,2,1,0:T(8,128)(2,1)S(1)} async-done(((bf16[32,3,48,128]{3,2,1,0:T(8,128)(2,1)}), bf16[32,3,48,128]{3,2,1,0:T(8,128)(2,1)S(1)}, u32[]{:S(2)}, u32[]{:S(2)}) %all-to-all-start.2) | async-done | bytes 1179680 | tf_op jit(solution)/shard_map/all_to_all | solution.py:398
  118.7 8.9 %finish.1 = (bf16[8,16,3072]{2,1,0:T(8,128)(2,1)}, bf16[8,32,3072]{2,1,0:T(8,128)(2,1)}, f32[8,32,64]{2,1,0:T(8,128)}) custom-call(bf16[8,2,2,3,48,128]{5,4,3,2,1,0:T(8,128)(2,1)S(1)} %bitcast.9, bf16[3,2,128,3072]{3,2,1,0:T(8,128)(2,1)} %bitcast.18, bf16[3,2,128,3072]{3,2,1,0:T(8,128)(2,1)} %collective-permute-done.2.other_w, ...), custom_call_target="tpu_custom_call" | custom-call | flops 3623878656 | bytes 18874368 | tf_op jit(solution)/shard_map/finish/pallas_call | solution.py:321
  (1 shorter events, 0.0 us)
Async XLA Ops:
  0.6 5.9 %copy-start.4 = (s32[32,3]{0,1:T(4,128)S(1)}, s32[32,3]{0,1:T(4,128)}, u32[]{:S(2)}) copy-start(s32[32,3]{0,1:T(4,128)} %param.19) | copy-start | bytes 1156
  0.6 6.3 %copy-start.2 = (f32[3,128]{1,0:T(4,128)S(1)}, f32[3,128]{1,0:T(4,128)}, u32[]{:S(2)}) copy-start(f32[3,128]{1,0:T(4,128)} %constant.2.clone.refs_5_.refs_3_) | copy-start | bytes 4612
  0.7 6.3 %copy-start.3 = (f32[2,128]{1,0:T(2,128)S(1)}, f32[2,128]{1,0:T(2,128)}, u32[]{:S(2)}) copy-start(f32[2,128]{1,0:T(2,128)} %refs_4_.3) | copy-start | bytes 3076
  6.4 7.0 %collective-permute-start = (bf16[8,48,3072]{2,1,0:T(8,128)(2,1)S(1)}, bf16[8,48,3072]{2,1,0:T(8,128)(2,1)S(1)}, u32[]{:S(2)}, u32[]{:S(2)}) collective-permute-start(bf16[8,48,3072]{2,1,0:T(8,128)(2,1)S(1)} %norm_tokens.1.refs_0_), channel_id=1, source_target_pairs={{0,1},{1,0},{2,3},{3,2},{4,5},{5,4},{6,7},{7,6},{8,9},{9,8},{10,11... | collective-permute-start | bytes 7077896 | tf_op jit(solution)/shard_map/ppermute | solution.py:380
  6.5 6.9 %collective-permute-start.1 = (s32[3,32]{1,0:T(4,128)S(1)}, s32[3,32]{1,0:T(4,128)S(1)}, u32[]{:S(2)}, u32[]{:S(2)}) collective-permute-start(s32[3,32]{1,0:T(4,128)S(1)} %bitcast.10), channel_id=1, source_target_pairs={{0,1},{1,0},{2,3},{3,2},{4,5},{5,4},{6,7},{7,6},{8,9},{9,8},{10,11... | collective-permute-start | bytes 1160 | tf_op jit(solution)/shard_map/ppermute | solution.py:381
  13.4 7.2 %copy-start = (bf16[8,48,3072]{2,1,0:T(8,128)(2,1)}, bf16[8,48,3072]{2,1,0:T(8,128)(2,1)S(1)}, u32[]{:S(2)}) copy-start(bf16[8,48,3072]{2,1,0:T(8,128)(2,1)S(1)} %collective-permute-done.refs_1_.refs_0_) | copy-start | bytes 7077892
  20.6 27.7 %all-to-all-start.1 = ((bf16[16,3,96,128]{3,2,1,0:T(8,128)(2,1)}), bf16[16,3,96,128]{3,2,1,0:T(8,128)(2,1)S(1)}, u32[]{:S(2)}, u32[]{:S(2)}) async-start(bf16[16,3,96,128]{3,2,1,0:T(8,128)(2,1)} %bitcast.16), calls=%async_computation.1 | async-start | bytes 2359296 | tf_op jit(solution)/shard_map/all_to_all | solution.py:386
  28.8 71.2 %collective-permute-start.2 = (bf16[3,2,128,3072]{3,2,1,0:T(8,128)(2,1)}, bf16[3,2,128,3072]{3,2,1,0:T(8,128)(2,1)}, u32[]{:S(2)}, u32[]{:S(2)}) collective-permute-start(bf16[3,2,128,3072]{3,2,1,0:T(8,128)(2,1)} %bitcast.17), channel_id=1, source_target_pairs={{0,1},{1,0},{2,3},{3,2},{4,5},{5,4},{6,7},{7,6},{8,9},{9,8},{10,11... | collective-permute-start | bytes 14155784 | tf_op jit(solution)/shard_map/ppermute | solution.py:382
  29.1 1.7 %copy-start.1 = (bf16[8,48,3072]{2,1,0:T(8,128)(2,1)S(1)}, bf16[8,48,3072]{2,1,0:T(8,128)(2,1)}, u32[]{:S(2)}) copy-start(bf16[8,48,3072]{2,1,0:T(8,128)(2,1)} %copy-done) | copy-start | bytes 7077892
  48.3 4.1 %copy-start.5 = (s32[8,16]{1,0:T(8,128)S(1)}, s32[8,16]{1,0:T(8,128)}, u32[]{:S(2)}) copy-start(s32[8,16]{1,0:T(8,128)} %keep_ref.3) | copy-start | bytes 1540
  48.3 4.1 %copy-start.6 = (s32[8]{0:T(128)S(1)}, s32[8]{0:T(128)}, u32[]{:S(2)}) copy-start(s32[8]{0:T(128)} %used_ref.3) | copy-start | bytes 100
  48.4 38.6 %all-to-all-start = ((bf16[16,6,96,128]{3,2,1,0:T(8,128)(2,1)}), bf16[16,6,96,128]{3,2,1,0:T(8,128)(2,1)S(1)}, u32[]{:S(2)}, u32[]{:S(2)}) async-start(bf16[16,6,96,128]{3,2,1,0:T(8,128)(2,1)} %bitcast.19), calls=%async_computation | async-start | bytes 4718592 | tf_op jit(solution)/shard_map/all_to_all | solution.py:386
  95.8 23.0 %all-to-all-start.2 = ((bf16[32,3,48,128]{3,2,1,0:T(8,128)(2,1)}), bf16[32,3,48,128]{3,2,1,0:T(8,128)(2,1)S(1)}, u32[]{:S(2)}, u32[]{:S(2)}) async-start(bf16[32,3,48,128]{3,2,1,0:T(8,128)(2,1)} %bitcast.22), calls=%async_computation.2 | async-start | bytes 2359296 | tf_op jit(solution)/shard_map/all_to_all | solution.py:398

commit v3 on v2

v3 whole, which is shorter than its diff:
```python
import functools
import math

import jax
import jax.numpy as jnp
import numpy as np
from jax import lax
from jax.experimental import pallas as pl
from jax.experimental.pallas import tpu as pltpu
from jax.sharding import PartitionSpec as P

eps_norm = 1e-06
theta_base = 10000.0
step_size = -0.25
excluded = -1e30
extra_rows = 16
MIB = 1 << 20
F32 = jnp.float32
BF16 = jnp.bfloat16


def in_hbm(array):
    return pltpu.with_memory_space_constraint(array, pltpu.HBM)


def in_vmem():
    return pl.BlockSpec(memory_space=pltpu.VMEM)


def in_place():
    return pl.BlockSpec(memory_space=pl.ANY)


def rope_rates(head_dim):
    half = head_dim // 2
    first = head_dim // 16
    second = (half - first) // 2
    counts = [first, second, half - first - second]
    tables = []
    for axis_id in range(3):
        pieces = []
        for other in range(3):
            if other == axis_id:
                pieces.append(theta_base ** (-np.arange(counts[other]) / counts[other]))
            else:
                pieces.append(np.zeros(counts[other]))
        tables.append(np.concatenate(pieces + pieces).astype(np.float32))
    tables += [np.zeros_like(tables[0])] * (8 - len(tables))
    return np.stack(tables)


def layer_norm(values):
    center = values - jnp.mean(values, axis=-1, keepdims=True)
    return center * lax.rsqrt(jnp.mean(center * center, axis=-1, keepdims=True) + eps_norm)


def norm_kernel(text_hbm, img_hbm, mod_hbm, w_hbm, pos_ref, out_ref, w_ref, text, img, mod, sems):
    samples, text_rows, _ = text.shape
    rows = text_rows + img.shape[1]
    columns = w_ref.shape[1] // 3
    mod_copy = pltpu.make_async_copy(mod_hbm.at[pl.ds(0, 2)], mod, sems.at[0])
    mod_copy.start()
    copies = []
    for s in range(samples):
        copies.append(
            (
                pltpu.make_async_copy(text_hbm.at[s], text.at[s], sems.at[1 + 2 * s]),
                pltpu.make_async_copy(img_hbm.at[s], img.at[s], sems.at[2 + 2 * s]),
            )
        )
        for copy in copies[-1]:
            copy.start()
    fetches = []
    for t in range(3):
        fetches.append(
            pltpu.make_async_copy(
                w_hbm.at[t, :, pl.ds(0, columns)],
                w_ref.at[:, pl.ds(t * columns, columns)],
                sems.at[1 + 2 * samples + t],
            )
        )
        fetches[-1].start()
    img_rows = pos_ref.shape[1]
    ids = jnp.zeros((extra_rows, img_rows), F32)
    row = lax.broadcasted_iota(jnp.int32, ids.shape, 0)
    for axis_id in range(pos_ref.shape[0]):
        ids = jnp.where(row == axis_id, pos_ref[axis_id : axis_id + 1, :].astype(F32), ids)
    out_ref[samples * rows :] = jnp.zeros((extra_rows, out_ref.shape[1]), BF16)
    out_ref[samples * rows :, :img_rows] = ids.astype(BF16)
    mod_copy.wait()
    for s in range(samples):
        for copy in copies[s]:
            copy.wait()
        shift = mod[0, s : s + 1, :]
        scale = 1.0 + mod[1, s : s + 1, :]
        begin, middle = s * rows, s * rows + text_rows
        text_norm = scale * layer_norm(text[s].astype(F32)) + shift
        out_ref[begin:middle] = text_norm.astype(BF16)
        img_norm = scale * layer_norm(img[s].astype(F32)) + shift
        out_ref[middle : begin + rows] = img_norm.astype(BF16)
    for fetch in fetches:
        fetch.wait()


def norm_tokens(text_hidden, img_hidden, mod, w_qkv, pos, head_dim):
    samples, text_rows, width = text_hidden.shape
    rows = text_rows + img_hidden.shape[1]
    return pl.pallas_call(
        norm_kernel,
        in_specs=[in_place()] * 4 + [in_vmem()],
        out_specs=[in_vmem(), in_vmem()],
        out_shape=[
            jax.ShapeDtypeStruct((samples * rows + extra_rows, width), BF16),
            jax.ShapeDtypeStruct((width, 6 * head_dim), BF16),
        ],
        scratch_shapes=[
            pltpu.VMEM(text_hidden.shape, BF16),
            pltpu.VMEM(img_hidden.shape, BF16),
            pltpu.VMEM((2, samples, width), F32),
            pltpu.SemaphoreType.DMA((4 + 2 * samples,)),
        ],
        compiler_params=pltpu.CompilerParams(vmem_limit_bytes=16 * MIB),
        cost_estimate=pl.CostEstimate(
            flops=samples * rows * width * 10,
            bytes_accessed=samples * rows * width * 4,
            transcendentals=0,
        ),
        name="norm_tokens",
    )(in_hbm(text_hidden), in_hbm(img_hidden), in_hbm(mod), in_hbm(w_qkv), pos)


def qkv_kernel(*refs, sides, jobs, ready, samples, img_rows):
    x_refs = refs[: len(sides)]
    w_hbm, rates_ref, gain_ref = refs[len(sides) : len(sides) + 3]
    out_hbm, w_buf, stage, w_sems, out_sems = refs[-5:]
    tokens = x_refs[0].shape[0] - extra_rows
    rows = tokens // samples
    head_dim = gain_ref.shape[1]
    col = lax.axis_index("col")
    wide = 2 * head_dim
    pairs = [pair for pair in sorted({job[1] for job in jobs}) if pair != ready]
    loads = {}
    for n, pair in enumerate(pairs):
        loads[pair] = [
            pltpu.make_async_copy(
                w_hbm.at[t, :, pl.ds(pair * wide, wide)],
                w_buf.at[n, :, pl.ds(t * wide, wide)],
                w_sems.at[3 * n + t],
            )
            for t in range(3)
        ]
        for load in loads[pair]:
            load.start()
    turns = []
    for x_ref in x_refs:
        ids = x_ref[tokens:, :128].astype(F32)[: rates_ref.shape[0], :img_rows]
        angle = lax.dot_general(
            ids, rates_ref[...], (((0,), (0,)), ((), ())),
            precision=lax.Precision.HIGHEST, preferred_element_type=F32,
        )
        angle = jnp.concatenate([jnp.zeros((rows - img_rows, head_dim), F32), angle], axis=0)
        lane = lax.broadcasted_iota(jnp.int32, angle.shape, 1)
        sine = jnp.sin(angle)
        turns.append((jnp.cos(angle), jnp.where(lane < head_dim // 2, -sine, sine)))
    stores = []
    for slot, (side, pair, base, placed) in enumerate(jobs):
        which = sides.index(side)
        if pair == ready:
            w_ref = refs[len(sides) + 3]
        else:
            w_ref = w_buf.at[pairs.index(pair)]
            for load in loads.pop(pair, []):
                load.wait()
        y = jnp.dot(x_refs[which][:tokens], w_ref[...], preferred_element_type=F32)
        cosine, sine = turns[which]
        for t in range(3):
            for hh in range(2):
                at = t * wide + hh * head_dim
                v = y[:, at : at + head_dim]
                if t < 2:
                    v = v * lax.rsqrt(jnp.mean(v * v, axis=-1, keepdims=True) + eps_norm)
                    v = v * gain_ref[t : t + 1, :]
                    rolled = pltpu.roll(v, head_dim // 2, 1).reshape(samples, rows, head_dim)
                    v = v.reshape(samples, rows, head_dim) * cosine[None] + rolled * sine[None]
                stage[slot, :, hh, t] = v.reshape(samples, rows, head_dim).astype(BF16)
        place = col if side == 0 else 1 - col
        begin = base + 3 * place if placed else base
        stores.append(
            pltpu.make_async_copy(
                stage.at[slot], out_hbm.at[:, :, pl.ds(begin, 3)], out_sems.at[slot]
            )
        )
        stores[-1].start()
    for store in stores:
        store.wait()


def qkv_heads(xs, sides, w_qkv, gain, samples, img_rows, first_w, jobs, slots, before=None):
    width = xs[0].shape[1]
    rows = (xs[0].shape[0] - extra_rows) // samples
    head_dim = gain.shape[1]
    operands = [*xs, in_hbm(w_qkv), rope_rates(head_dim), gain]
    in_specs = [in_vmem() for _ in operands]
    in_specs[len(xs)] = in_place()
    if first_w is not None:
        operands.append(first_w)
        in_specs.append(in_vmem())
    if before is not None:
        operands.append(in_hbm(before))
        in_specs.append(in_place())
    fetched = max(1, len({job[1] for job in jobs}) - (first_w is not None))
    return pl.pallas_call(
        functools.partial(
            qkv_kernel, sides=sides, jobs=jobs, samples=samples, img_rows=img_rows,
            ready=-1 if first_w is None else jobs[0][1],
        ),
        in_specs=in_specs,
        out_specs=in_place(),
        out_shape=pltpu.HBM((samples, 2, slots, rows, head_dim), BF16),
        input_output_aliases={} if before is None else {len(operands) - 1: 0},
        scratch_shapes=[
            pltpu.VMEM((fetched, width, 6 * head_dim), BF16),
            pltpu.VMEM((len(jobs), samples, 2, 3, rows, head_dim), BF16),
            pltpu.SemaphoreType.DMA((3 * fetched,)),
            pltpu.SemaphoreType.DMA((len(jobs),)),
        ],
        compiler_params=pltpu.CompilerParams(vmem_limit_bytes=24 * MIB),
        cost_estimate=pl.CostEstimate(
            flops=2 * samples * rows * width * 6 * len(jobs) * head_dim,
            bytes_accessed=2 * (len(xs) * samples * rows * width + width * 6 * head_dim),
            transcendentals=0,
        ),
        name="qkv_heads",
    )(*operands)


def attend_kernel(*refs, arrays, heads, samples, text_rows, step):
    used_ref, keep_ref = refs[:2]
    packed = refs[2 : 2 + arrays]
    out_hbm, wide_q, wide_k, wide_v, stage, sems = refs[-6:]
    tiles, _, rows, _ = wide_q.shape
    head_dim = packed[0].shape[-1]
    factor = math.log2(math.e) / math.sqrt(head_dim)
    col = lax.axis_index("col")
    mine = lax.axis_index("row") // (tiles // samples)
    used = used_ref[mine]
    at = lax.broadcasted_iota(jnp.int32, (rows, head_dim), 0)
    for r in range(tiles):
        img_bias = jnp.where(keep_ref[mine, r] > 0, 0.0, excluded)
        for half in range(2):
            text_at = at + (2 * r + half) * text_rows
            text_bias = jnp.where(text_at < used, 0.0, excluded)
            bias = jnp.where(at < text_rows, text_bias, img_bias)
            wide_k[r, half, :, head_dim:] = bias.astype(BF16)
    lane = lax.broadcasted_iota(jnp.int32, (tiles, 2, rows, head_dim), 3)
    wide_q[:, :, :, head_dim:] = jnp.where(lane == 0, 1.0, 0.0).astype(BF16)
    wide_v[:, :, :, head_dim:] = jnp.ones((tiles, 2, rows, head_dim), BF16)
    stores = []
    for n, (place, parts) in enumerate(heads):
        for array, slot, half in parts:
            half = col if half is None else 1 - col if half < 0 else half
            for t, wide in enumerate((wide_q, wide_k, wide_v)):
                wide[:, half, :, :head_dim] = packed[array][:, slot + t]
        keys = wide_k[...].reshape(tiles * 2 * rows, 2 * head_dim)
        values = wide_v[...].reshape(tiles * 2 * rows, 2 * head_dim)
        for r in range(0, tiles, step):
            scores = lax.dot_general(
                wide_q[r : r + step].reshape(step * 2 * rows, 2 * head_dim),
                keys,
                (((1,), (1,)), ((), ())),
                preferred_element_type=F32,
            )
            top = jnp.max(scores, axis=-1, keepdims=True)
            weights = jnp.exp2((scores - top) * factor).astype(BF16)
            summed = jnp.dot(weights, values, preferred_element_type=F32)
            result = (summed[:, :head_dim] / summed[:, head_dim:]).astype(BF16)
            stage[n, r : r + step] = result.reshape(step, 2, rows, head_dim)
        stores.append(pltpu.make_async_copy(stage.at[n], out_hbm.at[:, :, place], sems.at[n]))
        stores[-1].start()
    for store in stores:
        store.wait()


def attend(packed, heads, text_len, block_keep, before, text_rows, step, total):
    tiles, _, rows, head_dim = packed[0].shape
    tokens = tiles * 2 * rows
    samples = text_len.shape[0]
    smem = pl.BlockSpec(memory_space=pltpu.SMEM)
    operands = [text_len, block_keep, *packed]
    in_specs = [smem, smem] + [in_vmem()] * len(packed)
    if before is not None:
        operands.append(in_hbm(before))
        in_specs.append(in_place())
    return pl.pallas_call(
        functools.partial(
            attend_kernel, arrays=len(packed), heads=heads, samples=samples, text_rows=text_rows,
            step=step,
        ),
        in_specs=in_specs,
        out_specs=in_place(),
        out_shape=pltpu.HBM((tiles, 2, total, rows, head_dim), BF16),
        input_output_aliases={} if before is None else {len(operands) - 1: 0},
        scratch_shapes=[pltpu.VMEM((tiles, 2, rows, 2 * head_dim), BF16)] * 3
        + [
            pltpu.VMEM((len(heads), tiles, 2, rows, head_dim), BF16),
            pltpu.SemaphoreType.DMA((len(heads),)),
        ],
        compiler_params=pltpu.CompilerParams(vmem_limit_bytes=40 * MIB),
        cost_estimate=pl.CostEstimate(
            flops=8 * len(heads) * tokens * tokens * head_dim,
            bytes_accessed=2 * 4 * len(heads) * tokens * head_dim,
            transcendentals=len(heads) * tokens * tokens,
        ),
        name="attend",
    )(*operands)


def finish_kernel(
    att_ref, own_w, other_w, text, img, mod_hbm, wf_hbm, latent_hbm, text_hbm, img_hbm, next_ref,
    w_buf, mod, wf, latent, acc, final, text_new, img_new, sems,
):
    samples, _, _, heads, rows, head_dim = att_ref.shape
    width = own_w.shape[-1]
    text_rows, img_rows = text.shape[1], img.shape[1]
    col = lax.axis_index("col")
    one, rest = pl.ds(0, 1), pl.ds(1, heads - 1)
    loads = [
        (own_w.at[one], w_buf.at[0, one]),
        (own_w.at[rest], w_buf.at[0, rest]),
        (other_w, w_buf.at[1]),
        (mod_hbm, mod),
        (wf_hbm, wf),
        (latent_hbm, latent),
    ]
    loads = [pltpu.make_async_copy(a, b, sems.at[n]) for n, (a, b) in enumerate(loads)]
    for load in loads:
        load.start()

    def product(low, high, side, j_low, j_high):
        c = col if side == 0 else 1 - col
        pieces = [
            att_ref[low:high, hh, c, j].reshape((high - low) * rows, head_dim)
            for j in range(j_low, j_high)
            for hh in range(2)
        ]
        return jnp.dot(
            jnp.concatenate(pieces, axis=1),
            w_buf[side, j_low:j_high].reshape(2 * (j_high - j_low) * head_dim, width),
            preferred_element_type=F32,
        )

    loads[0].wait()
    acc[...] = product(0, samples, 0, 0, 1)
    loads[1].wait()
    acc[...] += product(0, samples, 0, 1, heads)
    for load in loads[2:]:
        load.wait()
    group = samples // 2
    stores = []
    for low in range(0, samples, group):
        acc[low * rows : (low + group) * rows] += product(low, low + group, 1, 0, heads)
        for s in range(low, low + group):
            gate = mod[2, s : s + 1, :]
            text_sum = acc[s * rows : s * rows + text_rows]
            text_new[s] = (text[s].astype(F32) + gate * text_sum).astype(BF16)
            img_sum = acc[s * rows + text_rows : (s + 1) * rows]
            new_img = (img[s].astype(F32) + gate * img_sum).astype(BF16)
            img_new[s] = new_img
            scaled = (1.0 + mod[4, s : s + 1, :]) * layer_norm(new_img.astype(F32))
            final[s * img_rows : (s + 1) * img_rows] = (scaled + mod[3, s : s + 1, :]).astype(BF16)
        part = pl.ds(low, group)
        for source, target in ((text_new, text_hbm), (img_new, img_hbm)):
            stores.append(
                pltpu.make_async_copy(
                    source.at[part], target.at[part], sems.at[len(loads) + len(stores)]
                )
            )
            stores[-1].start()
    velocity = lax.dot_general(
        final[...], wf[...], (((1,), (1,)), ((), ())), preferred_element_type=F32
    )
    next_ref[...] = latent[...] + step_size * velocity.reshape(latent.shape)
    for store in stores:
        store.wait()


def finish(att, own_w, other_w, text_hidden, img_hidden, mod, w_final, latent):
    samples, text_rows, width = text_hidden.shape
    img_rows = img_hidden.shape[1]
    rows = text_rows + img_rows
    near, far = in_vmem(), in_place()
    return pl.pallas_call(
        finish_kernel,
        in_specs=[near, far, far, near, near, far, far, far],
        out_specs=[far, far, near],
        out_shape=[
            pltpu.HBM(text_hidden.shape, BF16),
            pltpu.HBM(img_hidden.shape, BF16),
            pltpu.HBM(latent.shape, F32),
        ],
        scratch_shapes=[
            pltpu.VMEM((2, *own_w.shape), BF16),
            pltpu.VMEM(mod.shape, F32),
            pltpu.VMEM(w_final.shape, BF16),
            pltpu.VMEM(latent.shape, F32),
            pltpu.VMEM((samples * rows, width), F32),
            pltpu.VMEM((samples * img_rows, width), BF16),
            pltpu.VMEM(text_hidden.shape, BF16),
            pltpu.VMEM(img_hidden.shape, BF16),
            pltpu.SemaphoreType.DMA((10,)),
        ],
        compiler_params=pltpu.CompilerParams(vmem_limit_bytes=40 * MIB),
        cost_estimate=pl.CostEstimate(
            flops=4 * samples * rows * own_w.size,
            bytes_accessed=4 * own_w.size,
            transcendentals=0,
        ),
        name="finish",
    )(
        att, in_hbm(own_w), in_hbm(other_w), text_hidden, img_hidden, in_hbm(mod),
        in_hbm(w_final), in_hbm(latent),
    )


def per_device(
    img_hidden,
    text_hidden,
    latent,
    text_len,
    block_keep,
    img_pos,
    modulation,
    qk_gain,
    w_qkv,
    w_out,
    w_final,
):
    samples, img_rows, width = img_hidden.shape
    text_rows = text_hidden.shape[1]
    rows = text_rows + img_rows
    head_dim = qk_gain.shape[1]
    groups = w_out.shape[0] // (2 * head_dim)
    tiles = lax.axis_size("row")
    swap = [(0, 1), (1, 0)]
    mod = jnp.transpose(modulation, (1, 0, 2))
    w_heads = jnp.transpose(w_qkv, (1, 0, 2))
    own_w = w_out.reshape(groups, 2, head_dim, width)
    pos = jnp.transpose(img_pos)

    normed, first_w = norm_tokens(text_hidden, img_hidden, mod, w_heads, pos, head_dim)
    other_normed = lax.ppermute(normed, "col", swap)
    other_w = lax.ppermute(own_w, "col", swap)

    def exchange(mixed):
        mixed = mixed.reshape(tiles, mixed.shape[2], rows, head_dim)
        return lax.all_to_all(mixed, "row", 0, 0, tiled=True)

    sizes = (w_heads, qk_gain, samples, img_rows)
    both = ([normed, other_normed], (0, 1), *sizes)
    early = 1
    slots = 6 * early
    jobs = tuple((0, pair, 6 * pair, True) for pair in range(early))
    first = qkv_heads([normed], (0,), *sizes, first_w, jobs, slots)
    jobs = tuple((1, pair, 6 * pair, True) for pair in range(early))
    first = qkv_heads([other_normed], (1,), *sizes, first_w, jobs, slots, first)
    first = exchange(first)
    keys = (text_len, block_keep)

    def heads_of(low, high):
        return tuple((n, ((0, 6 * (n - low), 0), (0, 6 * (n - low) + 3, 1))) for n in range(low, high))

    jobs = tuple(
        (side, pair, 6 * (pair - early), True) for pair in range(early, groups) for side in range(2)
    )
    second = exchange(qkv_heads(*both, None, jobs, 6 * (groups - early)))
    attention = attend([first], heads_of(0, early), *keys, None, text_rows, 4, groups)
    attention = attend(
        [second], heads_of(early, groups), *keys, attention, text_rows, 4, groups
    )
    attention = attention.reshape(tiles * 2, groups, rows, head_dim)
    back = lax.all_to_all(attention, ("row", "col"), 0, 0, tiled=True)
    back = back.reshape(samples, 2, 2, groups, rows, head_dim)
    text_out, img_out, latent_next = finish(
        back, own_w, other_w, text_hidden, img_hidden, mod, jnp.transpose(w_final), latent
    )
    return (img_out, text_out, latent_next)


def solution(mesh):
    tokens = P("item", ("row", "col"), None)
    placed = (
        tokens,
        tokens,
        tokens,
        P("item"),
        P("item", None),
        P(("row", "col"), None),
        P("item", None, None),
        P(),
        P(None, None, "col"),
        P("col", None),
        P(),
    )
    return jax.shard_map(
        per_device,
        mesh=mesh,
        in_specs=placed,
        out_specs=(tokens, tokens, tokens),
        check_vma=False,
    )
```

time: 128 us -> 120 us (0.938)
  Pallas kernels: 55.4 us -> 43.9 us
  waiting for transfers between devices: 52.5 us -> 55 us
    pallas_call x7, Pallas kernels: 55.4 us -> 43.9 us  [the longest x3 18 us: qkv_heads(): pl.pallas_call(functools.partial(qkv_kernel, sides=sides, jobs=jobs, samp...]
    ppermute x1, waiting for transfers between devices: 0.01 us -> 1.47 us  [per_device(): other_normed = lax.ppermute(normed, 'col', swap)]
  transfers between devices with their start and end apart: 6 -> 5, of which waited for: 3 -> 4; matrix products, arithmetic and copies ran while one was open for 0% -> 0% of each run, Pallas kernels for 26% -> 24%
where the time goes in v3:
time: 120 us; the launch traced here: 119 us
  waiting for transfers between devices  55 us (46%)
  Pallas kernels  43.9 us (37%)
  starting transfers between devices  17 us (14%)
  local copies, waits for them, and re-layouts  2.39 us (2%)
    all_to_all x2, waiting for transfers between devices, exchange(): return lax.all_to_all(mixed, 'row', 0, 0, tiled=True)  34.8 us
    all_to_all x1, waiting for transfers between devices, per_device(): back = lax.all_to_all(attention, ('row', 'col'), 0, 0, tiled=True)  18.7 us
    pallas_call x3, Pallas kernels, qkv_heads(): pl.pallas_call(functools.partial(qkv_kernel, sides=sides, jobs=jobs, samp...  18 us
    pallas_call x2, Pallas kernels, attend(): pl.pallas_call(functools.partial(attend_kernel, arrays=len(packed), heads...  13.8 us
    all_to_all x2, starting transfers between devices, exchange(): return lax.all_to_all(mixed, 'row', 0, 0, tiled=True)  12.3 us
    pallas_call x1, Pallas kernels, finish(): pl.pallas_call(finish_kernel, in_specs=[near, far, far, near, near, far,...  8.45 us
    all_to_all x1, starting transfers between devices, per_device(): back = lax.all_to_all(attention, ('row', 'col'), 0, 0, tiled=True)  4.35 us
    pallas_call x1, Pallas kernels, norm_tokens(): pl.pallas_call(norm_kernel, in_specs=[in_place()] * 4 + [in_vmem()], out_...  3.68 us
  transfers between devices with their start and end apart: 5, of which 4 were waited for; matrix products, arithmetic and copies ran while one was open for 0% of the time, Pallas kernels for 24%

profile of v3, /device:TPU:0, one launch (start us, length us, event | category | flops | bytes accessed | tf_op | source)
XLA Modules:
  0.0 119.3 jit_solution(7108350313931632019)
XLA Ops:
  0.6 0.0 copy-start.6
  0.6 0.7 copy-done.6
  1.3 0.0 copy-start.4
  1.3 0.0 copy-start.5
  1.3 3.7 %norm_tokens.1 = (bf16[400,3072]{1,0:T(8,128)(2,1)S(1)}, bf16[3072,768]{1,0:T(8,128)(2,1)S(1)}) custom-call(bf16[8,16,3072]{2,1,0:T(8,128)(2,1)} %text.1, bf16[8,32,3072]{2,1,0:T(8,128)(2,1)} %img.1, f32[5,8,3072]{2,1,0:T(8,128)} %bitcast.19, bf16[3,3072,768]{2,1,0:T(8,128)(2,1)} %bitcast.11, s32[3,32]{1,0:T(4,128)S(1)} %bitcast.10), custom_call_target="tpu_custom_call" | custom-call | flops 11796480 | bytes 4718592 | tf_op jit(solution)/shard_map/norm_tokens/pallas_call | solution.py:108
  5.0 0.1 collective-permute-start
  5.1 0.0 copy-done.4
  5.1 0.0 copy-done.5
  5.1 3.2 %qkv_heads.4.refs_5_ = bf16[8,2,6,48,128]{4,3,2,1,0:T(8,128)(2,1)} custom-call(bf16[400,3072]{1,0:T(8,128)(2,1)S(1)} %get-tuple-element.8.refs_0_, bf16[3,3072,768]{2,1,0:T(8,128)(2,1)} %bitcast.12, f32[8,128]{1,0:T(8,128)S(1)} %copy-done.4, f32[2,128]{1,0:T(2,128)S(1)} %copy-done.5, bf16[3072,768]{1,0:T(8,128)(2,1)S(1)} %get-tuple-element.9.refs_4_), custom_call_target="tpu_custom_call" | custom-call | flops 1811939328 | bytes 7077888 | tf_op jit(solution)/shard_map/qkv_heads/pallas_call | solution.py:212
  8.3 1.5 %collective-permute-done.refs_1_.refs_0_ = bf16[400,3072]{1,0:T(8,128)(2,1)S(1)} collective-permute-done((bf16[400,3072]{1,0:T(8,128)(2,1)S(1)}, bf16[400,3072]{1,0:T(8,128)(2,1)S(1)}, u32[]{:S(2)}, u32[]{:S(2)}) %collective-permute-start) | collective-permute-done | bytes 2457632 | tf_op jit(solution)/shard_map/ppermute | solution.py:451
  9.8 3.2 %qkv_heads.5 = bf16[8,2,6,48,128]{4,3,2,1,0:T(8,128)(2,1)} custom-call(bf16[400,3072]{1,0:T(8,128)(2,1)S(1)} %collective-permute-done.refs_1_.refs_0_, bf16[3,3072,768]{2,1,0:T(8,128)(2,1)} %bitcast.13, f32[8,128]{1,0:T(8,128)S(1)} %copy-done.4, f32[2,128]{1,0:T(2,128)S(1)} %copy-done.5, ...), custom_call_target="tpu_custom_call", output_to_operand_aliasing={{}: (5, {})} | custom-call | flops 1811939328 | bytes 7077888 | tf_op jit(solution)/shard_map/qkv_heads/pallas_call | solution.py:212
  12.9 0.0 copy-done.2
  12.9 8.2 %all-to-all-start.1 = ((bf16[16,6,48,128]{3,2,1,0:T(8,128)(2,1)}), bf16[16,6,48,128]{3,2,1,0:T(8,128)(2,1)}, u32[]{:S(2)}, u32[]{:S(2)}) async-start(bf16[16,6,48,128]{3,2,1,0:T(8,128)(2,1)} %bitcast.15), calls=%async_computation.1 | async-start | bytes 2359296 | tf_op jit(solution)/shard_map/all_to_all | solution.py:456
  21.1 0.3 collective-permute-start.1
  21.4 0.0 copy-start.3
  21.4 1.7 %copy-done.3 = bf16[400,3072]{1,0:T(8,128)(2,1)S(1)} copy-done((bf16[400,3072]{1,0:T(8,128)(2,1)S(1)}, bf16[400,3072]{1,0:T(8,128)(2,1)}, u32[]{:S(2)}) %copy-start.3) | copy-done | bytes 2457624
  23.1 11.7 %qkv_heads.3 = bf16[8,2,12,48,128]{4,3,2,1,0:T(8,128)(2,1)} custom-call(bf16[400,3072]{1,0:T(8,128)(2,1)S(1)} %get-tuple-element.8.refs_0_, bf16[400,3072]{1,0:T(8,128)(2,1)S(1)} %copy-done.3, bf16[3,3072,768]{2,1,0:T(8,128)(2,1)} %bitcast.14, f32[8,128]{1,0:T(8,128)S(1)} %copy-done.4, f32[2,128]{1,0:T(2,128)S(1)} %copy-done.5), custom_call_target="tpu_custom_call" | custom-call | flops 7247757312 | bytes 9437184 | tf_op jit(solution)/shard_map/qkv_heads/pallas_call | solution.py:212
  34.8 6.1 %all-to-all-done.1.refs_2_ = bf16[16,6,48,128]{3,2,1,0:T(8,128)(2,1)} async-done(((bf16[16,6,48,128]{3,2,1,0:T(8,128)(2,1)}), bf16[16,6,48,128]{3,2,1,0:T(8,128)(2,1)}, u32[]{:S(2)}, u32[]{:S(2)}) %all-to-all-start.1) | async-done | bytes 1179680 | tf_op jit(solution)/shard_map/all_to_all | solution.py:456
  40.9 4.1 %all-to-all-start = ((bf16[16,12,48,128]{3,2,1,0:T(8,128)(2,1)}), bf16[16,12,48,128]{3,2,1,0:T(8,128)(2,1)S(1)}, u32[]{:S(2)}, u32[]{:S(2)}) async-start(bf16[16,12,48,128]{3,2,1,0:T(8,128)(2,1)} %bitcast.18), calls=%async_computation | async-start | bytes 4718592 | tf_op jit(solution)/shard_map/all_to_all | solution.py:456
  44.9 0.0 copy-done.7
  45.0 0.0 copy-done.8
  45.0 5.7 %attend.2.refs_3_ = bf16[16,2,3,48,128]{4,3,2,1,0:T(8,128)(2,1)} custom-call(s32[8]{0:T(128)S(1)} %copy-done.8, s32[8,16]{1,0:T(8,128)S(1)} %copy-done.7, bf16[16,6,48,128]{3,2,1,0:T(8,128)(2,1)} %all-to-all-done.1.refs_2_), custom_call_target="tpu_custom_call" | custom-call | flops 2415919104 | bytes 1572864 | tf_op jit(solution)/shard_map/attend/pallas_call | solution.py:294
  50.7 28.7 %all-to-all-done.refs_2_ = bf16[16,12,48,128]{3,2,1,0:T(8,128)(2,1)S(1)} async-done(((bf16[16,12,48,128]{3,2,1,0:T(8,128)(2,1)}), bf16[16,12,48,128]{3,2,1,0:T(8,128)(2,1)S(1)}, u32[]{:S(2)}, u32[]{:S(2)}) %all-to-all-start) | async-done | bytes 2359328 | tf_op jit(solution)/shard_map/all_to_all | solution.py:456
  79.4 8.1 %attend.3 = bf16[16,2,3,48,128]{4,3,2,1,0:T(8,128)(2,1)} custom-call(s32[8]{0:T(128)S(1)} %copy-done.8, s32[8,16]{1,0:T(8,128)S(1)} %copy-done.7, bf16[16,12,48,128]{3,2,1,0:T(8,128)(2,1)S(1)} %all-to-all-done.refs_2_, bf16[16,2,3,48,128]{4,3,2,1,0:T(8,128)(2,1)} %attend.2.refs_3_), custom_call_target="tpu_custom_call", output_to_operand_aliasing={{}: (3, {})} | custom-call | flops 4831838208 | bytes 3145728 | tf_op jit(solution)/shard_map/attend/pallas_call | solution.py:294
  87.5 0.0 copy-start
  87.5 0.0 copy-start.1
  87.5 4.3 %all-to-all-start.2 = ((bf16[32,3,48,128]{3,2,1,0:T(8,128)(2,1)}), bf16[32,3,48,128]{3,2,1,0:T(8,128)(2,1)S(1)}, u32[]{:S(2)}, u32[]{:S(2)}) async-start(bf16[32,3,48,128]{3,2,1,0:T(8,128)(2,1)} %bitcast.21), calls=%async_computation.2 | async-start | bytes 2359296 | tf_op jit(solution)/shard_map/all_to_all | solution.py:481
  91.9 0.0 collective-permute-done.1.other_w
  91.9 18.7 %all-to-all-done.2 = bf16[32,3,48,128]{3,2,1,0:T(8,128)(2,1)S(1)} async-done(((bf16[32,3,48,128]{3,2,1,0:T(8,128)(2,1)}), bf16[32,3,48,128]{3,2,1,0:T(8,128)(2,1)S(1)}, u32[]{:S(2)}, u32[]{:S(2)}) %all-to-all-start.2) | async-done | bytes 1179680 | tf_op jit(solution)/shard_map/all_to_all | solution.py:481
  110.6 0.0 copy-done
  110.6 0.0 copy-done.1
  110.6 8.4 %finish.1 = (bf16[8,16,3072]{2,1,0:T(8,128)(2,1)}, bf16[8,32,3072]{2,1,0:T(8,128)(2,1)}, f32[8,32,64]{2,1,0:T(8,128)}) custom-call(bf16[8,2,2,3,48,128]{5,4,3,2,1,0:T(8,128)(2,1)S(1)} %bitcast.9, bf16[3,2,128,3072]{3,2,1,0:T(8,128)(2,1)} %bitcast.17, bf16[3,2,128,3072]{3,2,1,0:T(8,128)(2,1)} %collective-permute-done.1.other_w, ...), custom_call_target="tpu_custom_call" | custom-call | flops 3623878656 | bytes 9437184 | tf_op jit(solution)/shard_map/finish/pallas_call | solution.py:392
  (3 shorter events, 0.0 us)
Async XLA Ops:
  0.6 0.7 copy-start.6
  1.3 3.8 %copy-start.4 = (f32[8,128]{1,0:T(8,128)S(1)}, f32[8,128]{1,0:T(8,128)}, u32[]{:S(2)}) copy-start(f32[8,128]{1,0:T(8,128)} %constant.2.clone.refs_3_.refs_2_) | copy-start | bytes 12292
  1.3 3.8 %copy-start.5 = (f32[2,128]{1,0:T(2,128)S(1)}, f32[2,128]{1,0:T(2,128)}, u32[]{:S(2)}) copy-start(f32[2,128]{1,0:T(2,128)} %refs_3_.4) | copy-start | bytes 3076
  5.0 4.8 %collective-permute-start = (bf16[400,3072]{1,0:T(8,128)(2,1)S(1)}, bf16[400,3072]{1,0:T(8,128)(2,1)S(1)}, u32[]{:S(2)}, u32[]{:S(2)}) collective-permute-start(bf16[400,3072]{1,0:T(8,128)(2,1)S(1)} %get-tuple-element.8.refs_0_), channel_id=1, source_target_pairs={{0,1},{1,0},{2,3},{3,2},{4,5},{5,4},{6,7},{7,6},{8,9},{9,8},{10,11... | collective-permute-start | bytes 7372808 | tf_op jit(solution)/shard_map/ppermute | solution.py:451
  9.8 3.2 %copy-start.2 = (bf16[400,3072]{1,0:T(8,128)(2,1)}, bf16[400,3072]{1,0:T(8,128)(2,1)S(1)}, u32[]{:S(2)}) copy-start(bf16[400,3072]{1,0:T(8,128)(2,1)S(1)} %collective-permute-done.refs_1_.refs_0_) | copy-start | bytes 7372804
  12.9 27.9 %all-to-all-start.1 = ((bf16[16,6,48,128]{3,2,1,0:T(8,128)(2,1)}), bf16[16,6,48,128]{3,2,1,0:T(8,128)(2,1)}, u32[]{:S(2)}, u32[]{:S(2)}) async-start(bf16[16,6,48,128]{3,2,1,0:T(8,128)(2,1)} %bitcast.15), calls=%async_computation.1 | async-start | bytes 2359296 | tf_op jit(solution)/shard_map/all_to_all | solution.py:456
  21.1 70.7 %collective-permute-start.1 = (bf16[3,2,128,3072]{3,2,1,0:T(8,128)(2,1)}, bf16[3,2,128,3072]{3,2,1,0:T(8,128)(2,1)}, u32[]{:S(2)}, u32[]{:S(2)}) collective-permute-start(bf16[3,2,128,3072]{3,2,1,0:T(8,128)(2,1)} %bitcast.16), channel_id=1, source_target_pairs={{0,1},{1,0},{2,3},{3,2},{4,5},{5,4},{6,7},{7,6},{8,9},{9,8},{10,11... | collective-permute-start | bytes 14155784 | tf_op jit(solution)/shard_map/ppermute | solution.py:452
  21.4 1.7 %copy-start.3 = (bf16[400,3072]{1,0:T(8,128)(2,1)S(1)}, bf16[400,3072]{1,0:T(8,128)(2,1)}, u32[]{:S(2)}) copy-start(bf16[400,3072]{1,0:T(8,128)(2,1)} %copy-done.2) | copy-start | bytes 7372804
  40.9 4.1 %copy-start.7 = (s32[8,16]{1,0:T(8,128)S(1)}, s32[8,16]{1,0:T(8,128)}, u32[]{:S(2)}) copy-start(s32[8,16]{1,0:T(8,128)} %refs_1_.3) | copy-start | bytes 1540
  40.9 4.1 %copy-start.8 = (s32[8]{0:T(128)S(1)}, s32[8]{0:T(128)}, u32[]{:S(2)}) copy-start(s32[8]{0:T(128)} %refs_0_.3) | copy-start | bytes 100
  40.9 38.5 %all-to-all-start = ((bf16[16,12,48,128]{3,2,1,0:T(8,128)(2,1)}), bf16[16,12,48,128]{3,2,1,0:T(8,128)(2,1)S(1)}, u32[]{:S(2)}, u32[]{:S(2)}) async-start(bf16[16,12,48,128]{3,2,1,0:T(8,128)(2,1)} %bitcast.18), calls=%async_computation | async-start | bytes 4718592 | tf_op jit(solution)/shard_map/all_to_all | solution.py:456
  87.5 23.1 %copy-start = (bf16[8,32,3072]{2,1,0:T(8,128)(2,1)S(1)}, bf16[8,32,3072]{2,1,0:T(8,128)(2,1)}, u32[]{:S(2)}) copy-start(bf16[8,32,3072]{2,1,0:T(8,128)(2,1)} %img.1) | copy-start | bytes 4718596
  87.5 23.1 %copy-start.1 = (bf16[8,16,3072]{2,1,0:T(8,128)(2,1)S(1)}, bf16[8,16,3072]{2,1,0:T(8,128)(2,1)}, u32[]{:S(2)}) copy-start(bf16[8,16,3072]{2,1,0:T(8,128)(2,1)} %text.1) | copy-start | bytes 2359300
  87.5 23.1 %all-to-all-start.2 = ((bf16[32,3,48,128]{3,2,1,0:T(8,128)(2,1)}), bf16[32,3,48,128]{3,2,1,0:T(8,128)(2,1)S(1)}, u32[]{:S(2)}, u32[]{:S(2)}) async-start(bf16[32,3,48,128]{3,2,1,0:T(8,128)(2,1)} %bitcast.21), calls=%async_computation.2 | async-start | bytes 2359296 | tf_op jit(solution)/shard_map/all_to_all | solution.py:481

commit v4 on v3

--- a/solution.py
+++ b/solution.py
@@ -54,12 +54,16 @@
     return center * lax.rsqrt(jnp.mean(center * center, axis=-1, keepdims=True) + eps_norm)
 
 
-def norm_kernel(text_hbm, img_hbm, mod_hbm, w_hbm, pos_ref, out_ref, w_ref, text, img, mod, sems):
+def norm_kernel(
+    text_hbm, img_hbm, mod_hbm, w_hbm, pos_hbm, out_ref, w_ref, text, img, mod, pos_ref, sems
+):
     samples, text_rows, _ = text.shape
     rows = text_rows + img.shape[1]
     columns = w_ref.shape[1] // 3
     mod_copy = pltpu.make_async_copy(mod_hbm.at[pl.ds(0, 2)], mod, sems.at[0])
     mod_copy.start()
+    pos_copy = pltpu.make_async_copy(pos_hbm, pos_ref, sems.at[4 + 2 * samples])
+    pos_copy.start()
     copies = []
     for s in range(samples):
         copies.append(
@@ -80,13 +84,6 @@
             )
         )
         fetches[-1].start()
-    img_rows = pos_ref.shape[1]
-    ids = jnp.zeros((extra_rows, img_rows), F32)
-    row = lax.broadcasted_iota(jnp.int32, ids.shape, 0)
-    for axis_id in range(pos_ref.shape[0]):
-        ids = jnp.where(row == axis_id, pos_ref[axis_id : axis_id + 1, :].astype(F32), ids)
-    out_ref[samples * rows :] = jnp.zeros((extra_rows, out_ref.shape[1]), BF16)
-    out_ref[samples * rows :, :img_rows] = ids.astype(BF16)
     mod_copy.wait()
     for s in range(samples):
         for copy in copies[s]:
@@ -98,6 +95,14 @@
         out_ref[begin:middle] = text_norm.astype(BF16)
         img_norm = scale * layer_norm(img[s].astype(F32)) + shift
         out_ref[middle : begin + rows] = img_norm.astype(BF16)
+    pos_copy.wait()
+    img_rows = pos_ref.shape[1]
+    ids = jnp.zeros((extra_rows, img_rows), F32)
+    row = lax.broadcasted_iota(jnp.int32, ids.shape, 0)
+    for axis_id in range(pos_ref.shape[0]):
+        ids = jnp.where(row == axis_id, pos_ref[axis_id : axis_id + 1, :].astype(F32), ids)
+    out_ref[samples * rows :] = jnp.zeros((extra_rows, out_ref.shape[1]), BF16)
+    out_ref[samples * rows :, :img_rows] = ids.astype(BF16)
     for fetch in fetches:
         fetch.wait()
 
@@ -107,7 +112,7 @@
     rows = text_rows + img_hidden.shape[1]
     return pl.pallas_call(
         norm_kernel,
-        in_specs=[in_place()] * 4 + [in_vmem()],
+        in_specs=[in_place()] * 5,
         out_specs=[in_vmem(), in_vmem()],
         out_shape=[
             jax.ShapeDtypeStruct((samples * rows + extra_rows, width), BF16),
@@ -117,7 +122,8 @@
             pltpu.VMEM(text_hidden.shape, BF16),
             pltpu.VMEM(img_hidden.shape, BF16),
             pltpu.VMEM((2, samples, width), F32),
-            pltpu.SemaphoreType.DMA((4 + 2 * samples,)),
+            pltpu.VMEM(pos.shape, jnp.int32),
+            pltpu.SemaphoreType.DMA((5 + 2 * samples,)),
         ],
         compiler_params=pltpu.CompilerParams(vmem_limit_bytes=16 * MIB),
         cost_estimate=pl.CostEstimate(
@@ -126,7 +132,7 @@
             transcendentals=0,
         ),
         name="norm_tokens",
-    )(in_hbm(text_hidden), in_hbm(img_hidden), in_hbm(mod), in_hbm(w_qkv), pos)
+    )(in_hbm(text_hidden), in_hbm(img_hidden), in_hbm(mod), in_hbm(w_qkv), in_hbm(pos))
 
 
 def qkv_kernel(*refs, sides, jobs, ready, samples, img_rows):
@@ -173,6 +179,8 @@
                 load.wait()
         y = jnp.dot(x_refs[which][:tokens], w_ref[...], preferred_element_type=F32)
         cosine, sine = turns[which]
+        place = col if side == 0 else 1 - col
+        begin = base + 3 * place if placed else base
         for t in range(3):
             for hh in range(2):
                 at = t * wide + hh * head_dim
@@ -182,15 +190,13 @@
                     v = v * gain_ref[t : t + 1, :]
                     rolled = pltpu.roll(v, head_dim // 2, 1).reshape(samples, rows, head_dim)
                     v = v.reshape(samples, rows, head_dim) * cosine[None] + rolled * sine[None]
-                stage[slot, :, hh, t] = v.reshape(samples, rows, head_dim).astype(BF16)
-        place = col if side == 0 else 1 - col
-        begin = base + 3 * place if placed else base
-        stores.append(
-            pltpu.make_async_copy(
-                stage.at[slot], out_hbm.at[:, :, pl.ds(begin, 3)], out_sems.at[slot]
+                stage[slot, t, :, hh] = v.reshape(samples, rows, head_dim).astype(BF16)
+            stores.append(
+                pltpu.make_async_copy(
+                    stage.at[slot, t], out_hbm.at[:, :, begin + t], out_sems.at[3 * slot + t]
+                )
             )
-        )
-        stores[-1].start()
+            stores[-1].start()
     for store in stores:
         store.wait()
 
@@ -220,9 +226,9 @@
         input_output_aliases={} if before is None else {len(operands) - 1: 0},
         scratch_shapes=[
             pltpu.VMEM((fetched, width, 6 * head_dim), BF16),
-            pltpu.VMEM((len(jobs), samples, 2, 3, rows, head_dim), BF16),
+            pltpu.VMEM((len(jobs), 3, samples, 2, rows, head_dim), BF16),
             pltpu.SemaphoreType.DMA((3 * fetched,)),
-            pltpu.SemaphoreType.DMA((len(jobs),)),
+            pltpu.SemaphoreType.DMA((3 * len(jobs),)),
         ],
         compiler_params=pltpu.CompilerParams(vmem_limit_bytes=24 * MIB),
         cost_estimate=pl.CostEstimate(
@@ -237,11 +243,10 @@
 def attend_kernel(*refs, arrays, heads, samples, text_rows, step):
     used_ref, keep_ref = refs[:2]
     packed = refs[2 : 2 + arrays]
-    out_hbm, wide_q, wide_k, wide_v, stage, sems = refs[-6:]
+    out_hbm, wide_q, wide_k, wide_v, all_scores, stage, sems = refs[-7:]
     tiles, _, rows, _ = wide_q.shape
     head_dim = packed[0].shape[-1]
     factor = math.log2(math.e) / math.sqrt(head_dim)
-    col = lax.axis_index("col")
     mine = lax.axis_index("row") // (tiles // samples)
     used = used_ref[mine]
     at = lax.broadcasted_iota(jnp.int32, (rows, head_dim), 0)
@@ -258,18 +263,17 @@
     stores = []
     for n, (place, parts) in enumerate(heads):
         for array, slot, half in parts:
-            half = col if half is None else 1 - col if half < 0 else half
             for t, wide in enumerate((wide_q, wide_k, wide_v)):
                 wide[:, half, :, :head_dim] = packed[array][:, slot + t]
-        keys = wide_k[...].reshape(tiles * 2 * rows, 2 * head_dim)
+        all_scores[...] = lax.dot_general(
+            wide_q[...].reshape(tiles * 2 * rows, 2 * head_dim),
+            wide_k[...].reshape(tiles * 2 * rows, 2 * head_dim),
+            (((1,), (1,)), ((), ())),
+            preferred_element_type=F32,
+        )
         values = wide_v[...].reshape(tiles * 2 * rows, 2 * head_dim)
         for r in range(0, tiles, step):
-            scores = lax.dot_general(
-                wide_q[r : r + step].reshape(step * 2 * rows, 2 * head_dim),
-                keys,
-                (((1,), (1,)), ((), ())),
-                preferred_element_type=F32,
-            )
+            scores = all_scores[r * 2 * rows : (r + step) * 2 * rows]
             top = jnp.max(scores, axis=-1, keepdims=True)
             weights = jnp.exp2((scores - top) * factor).astype(BF16)
             summed = jnp.dot(weights, values, preferred_element_type=F32)
@@ -302,6 +306,7 @@
         input_output_aliases={} if before is None else {len(operands) - 1: 0},
         scratch_shapes=[pltpu.VMEM((tiles, 2, rows, 2 * head_dim), BF16)] * 3
         + [
+            pltpu.VMEM((tokens, tokens), F32),
             pltpu.VMEM((len(heads), tiles, 2, rows, head_dim), BF16),
             pltpu.SemaphoreType.DMA((len(heads),)),
         ],

time: 120 us -> 118 us (0.983)
  Pallas kernels: 43.9 us -> 42.6 us
    pallas_call x2, Pallas kernels: 13.8 us -> 12.5 us  [attend(): pl.pallas_call(functools.partial(attend_kernel, arrays=len(packed), heads...]
  transfers between devices with their start and end apart: 5 -> 5, of which waited for: 4 -> 4; matrix products, arithmetic and copies ran while one was open for 0% -> 0% of each run, Pallas kernels for 24% -> 23%
where the time goes in v4:
time: 118 us
  waiting for transfers between devices  55.6 us (47%)
  Pallas kernels  42.6 us (36%)
  starting transfers between devices  17 us (14%)
  local copies, waits for them, and re-layouts  1.72 us (1%)
    all_to_all x2, waiting for transfers between devices, exchange(): return lax.all_to_all(mixed, 'row', 0, 0, tiled=True)  35.3 us
    all_to_all x1, waiting for transfers between devices, per_device(): back = lax.all_to_all(attention, ('row', 'col'), 0, 0, tiled=True)  18.7 us
    pallas_call x3, Pallas kernels, qkv_heads(): pl.pallas_call(functools.partial(qkv_kernel, sides=sides, jobs=jobs, samp...  17.9 us
    pallas_call x2, Pallas kernels, attend(): pl.pallas_call(functools.partial(attend_kernel, arrays=len(packed), heads...  12.5 us
    all_to_all x2, starting transfers between devices, exchange(): return lax.all_to_all(mixed, 'row', 0, 0, tiled=True)  12.3 us
    pallas_call x1, Pallas kernels, finish(): pl.pallas_call(finish_kernel, in_specs=[near, far, far, near, near, far,...  8.45 us
    all_to_all x1, starting transfers between devices, per_device(): back = lax.all_to_all(attention, ('row', 'col'), 0, 0, tiled=True)  4.35 us
    pallas_call x1, Pallas kernels, norm_tokens(): pl.pallas_call(norm_kernel, in_specs=[in_place()] * 5, out_specs=[in_vmem...  3.7 us
  transfers between devices with their start and end apart: 5, of which 4 were waited for; matrix products, arithmetic and copies ran while one was open for 0% of the time, Pallas kernels for 23%

profile of v4, /device:TPU:0, one launch (start us, length us, event | category | flops | bytes accessed | tf_op | source)
XLA Modules:
  0.0 117.9 jit_solution(5214938816882753912)
XLA Ops:
  0.6 0.0 copy-start.4
  0.6 0.0 copy-start.5
  0.7 3.7 %norm_tokens.1 = (bf16[400,3072]{1,0:T(8,128)(2,1)S(1)}, bf16[3072,768]{1,0:T(8,128)(2,1)S(1)}) custom-call(bf16[8,16,3072]{2,1,0:T(8,128)(2,1)} %text.1, bf16[8,32,3072]{2,1,0:T(8,128)(2,1)} %img.1, f32[5,8,3072]{2,1,0:T(8,128)} %bitcast.18, bf16[3,3072,768]{2,1,0:T(8,128)(2,1)} %bitcast.10, s32[3,32]{1,0:T(4,128)} %bitcast.22), custom_call_target="tpu_custom_call" | custom-call | flops 11796480 | bytes 4718592 | tf_op jit(solution)/shard_map/norm_tokens/pallas_call | solution.py:113
  4.4 0.1 collective-permute-start
  4.5 0.0 copy-done.4
  4.5 0.0 copy-done.5
  4.5 3.1 %qkv_heads.4.refs_5_ = bf16[8,2,6,48,128]{4,3,2,1,0:T(8,128)(2,1)} custom-call(bf16[400,3072]{1,0:T(8,128)(2,1)S(1)} %get-tuple-element.8.refs_0_, bf16[3,3072,768]{2,1,0:T(8,128)(2,1)} %bitcast.11, f32[8,128]{1,0:T(8,128)S(1)} %copy-done.4, f32[2,128]{1,0:T(2,128)S(1)} %copy-done.5, bf16[3072,768]{1,0:T(8,128)(2,1)S(1)} %get-tuple-element.9.refs_4_), custom_call_target="tpu_custom_call" | custom-call | flops 1811939328 | bytes 7077888 | tf_op jit(solution)/shard_map/qkv_heads/pallas_call | solution.py:218
  7.6 1.5 %collective-permute-done.refs_1_.refs_0_ = bf16[400,3072]{1,0:T(8,128)(2,1)S(1)} collective-permute-done((bf16[400,3072]{1,0:T(8,128)(2,1)S(1)}, bf16[400,3072]{1,0:T(8,128)(2,1)S(1)}, u32[]{:S(2)}, u32[]{:S(2)}) %collective-permute-start) | collective-permute-done | bytes 2457632 | tf_op jit(solution)/shard_map/ppermute | solution.py:456
  9.1 0.0 copy-start.2
  9.1 3.1 %qkv_heads.5 = bf16[8,2,6,48,128]{4,3,2,1,0:T(8,128)(2,1)} custom-call(bf16[400,3072]{1,0:T(8,128)(2,1)S(1)} %collective-permute-done.refs_1_.refs_0_, bf16[3,3072,768]{2,1,0:T(8,128)(2,1)} %bitcast.12, f32[8,128]{1,0:T(8,128)S(1)} %copy-done.4, f32[2,128]{1,0:T(2,128)S(1)} %copy-done.5, ...), custom_call_target="tpu_custom_call", output_to_operand_aliasing={{}: (5, {})} | custom-call | flops 1811939328 | bytes 7077888 | tf_op jit(solution)/shard_map/qkv_heads/pallas_call | solution.py:218
  12.2 0.0 copy-done.2
  12.2 8.2 %all-to-all-start.1 = ((bf16[16,6,48,128]{3,2,1,0:T(8,128)(2,1)}), bf16[16,6,48,128]{3,2,1,0:T(8,128)(2,1)}, u32[]{:S(2)}, u32[]{:S(2)}) async-start(bf16[16,6,48,128]{3,2,1,0:T(8,128)(2,1)} %bitcast.14), calls=%async_computation.1 | async-start | bytes 2359296 | tf_op jit(solution)/shard_map/all_to_all | solution.py:461
  20.4 0.3 collective-permute-start.1
  20.7 0.0 copy-start.3
  20.7 1.7 %copy-done.3 = bf16[400,3072]{1,0:T(8,128)(2,1)S(1)} copy-done((bf16[400,3072]{1,0:T(8,128)(2,1)S(1)}, bf16[400,3072]{1,0:T(8,128)(2,1)}, u32[]{:S(2)}) %copy-start.3) | copy-done | bytes 2457624
  22.4 11.7 %qkv_heads.3 = bf16[8,2,12,48,128]{4,3,2,1,0:T(8,128)(2,1)} custom-call(bf16[400,3072]{1,0:T(8,128)(2,1)S(1)} %get-tuple-element.8.refs_0_, bf16[400,3072]{1,0:T(8,128)(2,1)S(1)} %copy-done.3, bf16[3,3072,768]{2,1,0:T(8,128)(2,1)} %bitcast.13, f32[8,128]{1,0:T(8,128)S(1)} %copy-done.4, f32[2,128]{1,0:T(2,128)S(1)} %copy-done.5), custom_call_target="tpu_custom_call" | custom-call | flops 7247757312 | bytes 9437184 | tf_op jit(solution)/shard_map/qkv_heads/pallas_call | solution.py:218
  34.1 6.0 %all-to-all-done.1.refs_2_ = bf16[16,6,48,128]{3,2,1,0:T(8,128)(2,1)} async-done(((bf16[16,6,48,128]{3,2,1,0:T(8,128)(2,1)}), bf16[16,6,48,128]{3,2,1,0:T(8,128)(2,1)}, u32[]{:S(2)}, u32[]{:S(2)}) %all-to-all-start.1) | async-done | bytes 1179680 | tf_op jit(solution)/shard_map/all_to_all | solution.py:461
  40.2 0.0 copy-start.6
  40.2 4.1 %all-to-all-start = ((bf16[16,12,48,128]{3,2,1,0:T(8,128)(2,1)}), bf16[16,12,48,128]{3,2,1,0:T(8,128)(2,1)S(1)}, u32[]{:S(2)}, u32[]{:S(2)}) async-start(bf16[16,12,48,128]{3,2,1,0:T(8,128)(2,1)} %bitcast.17), calls=%async_computation | async-start | bytes 4718592 | tf_op jit(solution)/shard_map/all_to_all | solution.py:461
  44.2 0.0 copy-done.6
  44.3 0.0 copy-done.7
  44.3 5.1 %attend.2.refs_3_ = bf16[16,2,3,48,128]{4,3,2,1,0:T(8,128)(2,1)} custom-call(s32[8]{0:T(128)S(1)} %copy-done.7, s32[8,16]{1,0:T(8,128)S(1)} %copy-done.6, bf16[16,6,48,128]{3,2,1,0:T(8,128)(2,1)} %all-to-all-done.1.refs_2_), custom_call_target="tpu_custom_call" | custom-call | flops 2415919104 | bytes 1572864 | tf_op jit(solution)/shard_map/attend/pallas_call | solution.py:298
  49.4 29.3 %all-to-all-done.refs_2_ = bf16[16,12,48,128]{3,2,1,0:T(8,128)(2,1)S(1)} async-done(((bf16[16,12,48,128]{3,2,1,0:T(8,128)(2,1)}), bf16[16,12,48,128]{3,2,1,0:T(8,128)(2,1)S(1)}, u32[]{:S(2)}, u32[]{:S(2)}) %all-to-all-start) | async-done | bytes 2359328 | tf_op jit(solution)/shard_map/all_to_all | solution.py:461
  78.7 7.4 %attend.3 = bf16[16,2,3,48,128]{4,3,2,1,0:T(8,128)(2,1)} custom-call(s32[8]{0:T(128)S(1)} %copy-done.7, s32[8,16]{1,0:T(8,128)S(1)} %copy-done.6, bf16[16,12,48,128]{3,2,1,0:T(8,128)(2,1)S(1)} %all-to-all-done.refs_2_, bf16[16,2,3,48,128]{4,3,2,1,0:T(8,128)(2,1)} %attend.2.refs_3_), custom_call_target="tpu_custom_call", output_to_operand_aliasing={{}: (3, {})} | custom-call | flops 4831838208 | bytes 3145728 | tf_op jit(solution)/shard_map/attend/pallas_call | solution.py:298
  86.1 0.0 copy-start
  86.1 0.0 copy-start.1
  86.1 4.3 %all-to-all-start.2 = ((bf16[32,3,48,128]{3,2,1,0:T(8,128)(2,1)}), bf16[32,3,48,128]{3,2,1,0:T(8,128)(2,1)S(1)}, u32[]{:S(2)}, u32[]{:S(2)}) async-start(bf16[32,3,48,128]{3,2,1,0:T(8,128)(2,1)} %bitcast.20), calls=%async_computation.2 | async-start | bytes 2359296 | tf_op jit(solution)/shard_map/all_to_all | solution.py:486
  90.5 0.0 collective-permute-done.1.other_w
  90.5 18.7 %all-to-all-done.2 = bf16[32,3,48,128]{3,2,1,0:T(8,128)(2,1)S(1)} async-done(((bf16[32,3,48,128]{3,2,1,0:T(8,128)(2,1)}), bf16[32,3,48,128]{3,2,1,0:T(8,128)(2,1)S(1)}, u32[]{:S(2)}, u32[]{:S(2)}) %all-to-all-start.2) | async-done | bytes 1179680 | tf_op jit(solution)/shard_map/all_to_all | solution.py:486
  109.2 0.0 copy-done
  109.2 0.0 copy-done.1
  109.2 8.5 %finish.1 = (bf16[8,16,3072]{2,1,0:T(8,128)(2,1)}, bf16[8,32,3072]{2,1,0:T(8,128)(2,1)}, f32[8,32,64]{2,1,0:T(8,128)}) custom-call(bf16[8,2,2,3,48,128]{5,4,3,2,1,0:T(8,128)(2,1)S(1)} %bitcast.9, bf16[3,2,128,3072]{3,2,1,0:T(8,128)(2,1)} %bitcast.16, bf16[3,2,128,3072]{3,2,1,0:T(8,128)(2,1)} %collective-permute-done.1.other_w, ...), custom_call_target="tpu_custom_call" | custom-call | flops 3623878656 | bytes 9437184 | tf_op jit(solution)/shard_map/finish/pallas_call | solution.py:397
  (1 shorter events, 0.0 us)
Async XLA Ops:
  0.6 3.8 %copy-start.4 = (f32[8,128]{1,0:T(8,128)S(1)}, f32[8,128]{1,0:T(8,128)}, u32[]{:S(2)}) copy-start(f32[8,128]{1,0:T(8,128)} %constant.2.clone.refs_3_.refs_2_) | copy-start | bytes 12292
  0.6 3.8 %copy-start.5 = (f32[2,128]{1,0:T(2,128)S(1)}, f32[2,128]{1,0:T(2,128)}, u32[]{:S(2)}) copy-start(f32[2,128]{1,0:T(2,128)} %refs_3_.4) | copy-start | bytes 3076
  4.4 4.8 %collective-permute-start = (bf16[400,3072]{1,0:T(8,128)(2,1)S(1)}, bf16[400,3072]{1,0:T(8,128)(2,1)S(1)}, u32[]{:S(2)}, u32[]{:S(2)}) collective-permute-start(bf16[400,3072]{1,0:T(8,128)(2,1)S(1)} %get-tuple-element.8.refs_0_), channel_id=1, source_target_pairs={{0,1},{1,0},{2,3},{3,2},{4,5},{5,4},{6,7},{7,6},{8,9},{9,8},{10,11... | collective-permute-start | bytes 7372808 | tf_op jit(solution)/shard_map/ppermute | solution.py:456
  9.1 3.1 %copy-start.2 = (bf16[400,3072]{1,0:T(8,128)(2,1)}, bf16[400,3072]{1,0:T(8,128)(2,1)S(1)}, u32[]{:S(2)}) copy-start(bf16[400,3072]{1,0:T(8,128)(2,1)S(1)} %collective-permute-done.refs_1_.refs_0_) | copy-start | bytes 7372804
  12.2 27.9 %all-to-all-start.1 = ((bf16[16,6,48,128]{3,2,1,0:T(8,128)(2,1)}), bf16[16,6,48,128]{3,2,1,0:T(8,128)(2,1)}, u32[]{:S(2)}, u32[]{:S(2)}) async-start(bf16[16,6,48,128]{3,2,1,0:T(8,128)(2,1)} %bitcast.14), calls=%async_computation.1 | async-start | bytes 2359296 | tf_op jit(solution)/shard_map/all_to_all | solution.py:461
  20.4 70.0 %collective-permute-start.1 = (bf16[3,2,128,3072]{3,2,1,0:T(8,128)(2,1)}, bf16[3,2,128,3072]{3,2,1,0:T(8,128)(2,1)}, u32[]{:S(2)}, u32[]{:S(2)}) collective-permute-start(bf16[3,2,128,3072]{3,2,1,0:T(8,128)(2,1)} %bitcast.15), channel_id=1, source_target_pairs={{0,1},{1,0},{2,3},{3,2},{4,5},{5,4},{6,7},{7,6},{8,9},{9,8},{10,11... | collective-permute-start | bytes 14155784 | tf_op jit(solution)/shard_map/ppermute | solution.py:457
  20.7 1.7 %copy-start.3 = (bf16[400,3072]{1,0:T(8,128)(2,1)S(1)}, bf16[400,3072]{1,0:T(8,128)(2,1)}, u32[]{:S(2)}) copy-start(bf16[400,3072]{1,0:T(8,128)(2,1)} %copy-done.2) | copy-start | bytes 7372804
  40.2 4.1 %copy-start.6 = (s32[8,16]{1,0:T(8,128)S(1)}, s32[8,16]{1,0:T(8,128)}, u32[]{:S(2)}) copy-start(s32[8,16]{1,0:T(8,128)} %refs_1_.3) | copy-start | bytes 1540
  40.2 4.1 %copy-start.7 = (s32[8]{0:T(128)S(1)}, s32[8]{0:T(128)}, u32[]{:S(2)}) copy-start(s32[8]{0:T(128)} %refs_0_.3) | copy-start | bytes 100
  40.2 38.5 %all-to-all-start = ((bf16[16,12,48,128]{3,2,1,0:T(8,128)(2,1)}), bf16[16,12,48,128]{3,2,1,0:T(8,128)(2,1)S(1)}, u32[]{:S(2)}, u32[]{:S(2)}) async-start(bf16[16,12,48,128]{3,2,1,0:T(8,128)(2,1)} %bitcast.17), calls=%async_computation | async-start | bytes 4718592 | tf_op jit(solution)/shard_map/all_to_all | solution.py:461
  86.1 23.1 %copy-start = (bf16[8,32,3072]{2,1,0:T(8,128)(2,1)S(1)}, bf16[8,32,3072]{2,1,0:T(8,128)(2,1)}, u32[]{:S(2)}) copy-start(bf16[8,32,3072]{2,1,0:T(8,128)(2,1)} %img.1) | copy-start | bytes 4718596
  86.1 23.1 %copy-start.1 = (bf16[8,16,3072]{2,1,0:T(8,128)(2,1)S(1)}, bf16[8,16,3072]{2,1,0:T(8,128)(2,1)}, u32[]{:S(2)}) copy-start(bf16[8,16,3072]{2,1,0:T(8,128)(2,1)} %text.1) | copy-start | bytes 2359300
  86.1 23.1 %all-to-all-start.2 = ((bf16[32,3,48,128]{3,2,1,0:T(8,128)(2,1)}), bf16[32,3,48,128]{3,2,1,0:T(8,128)(2,1)S(1)}, u32[]{:S(2)}, u32[]{:S(2)}) async-start(bf16[32,3,48,128]{3,2,1,0:T(8,128)(2,1)} %bitcast.20), calls=%async_computation.2 | async-start | bytes 2359296 | tf_op jit(solution)/shard_map/all_to_all | solution.py:486

commit v5 on v4

--- a/solution.py
+++ b/solution.py
@@ -328,10 +328,8 @@
     width = own_w.shape[-1]
     text_rows, img_rows = text.shape[1], img.shape[1]
     col = lax.axis_index("col")
-    one, rest = pl.ds(0, 1), pl.ds(1, heads - 1)
     loads = [
-        (own_w.at[one], w_buf.at[0, one]),
-        (own_w.at[rest], w_buf.at[0, rest]),
+        (own_w, w_buf.at[0]),
         (other_w, w_buf.at[1]),
         (mod_hbm, mod),
         (wf_hbm, wf),
@@ -355,10 +353,8 @@
         )
 
     loads[0].wait()
-    acc[...] = product(0, samples, 0, 0, 1)
-    loads[1].wait()
-    acc[...] += product(0, samples, 0, 1, heads)
-    for load in loads[2:]:
+    acc[...] = product(0, samples, 0, 0, heads)
+    for load in loads[1:]:
         load.wait()
     group = samples // 2
     stores = []
@@ -478,9 +474,9 @@
         (side, pair, 6 * (pair - early), True) for pair in range(early, groups) for side in range(2)
     )
     second = exchange(qkv_heads(*both, None, jobs, 6 * (groups - early)))
-    attention = attend([first], heads_of(0, early), *keys, None, text_rows, 4, groups)
+    attention = attend([first], heads_of(0, early), *keys, None, text_rows, 8, groups)
     attention = attend(
-        [second], heads_of(early, groups), *keys, attention, text_rows, 4, groups
+        [second], heads_of(early, groups), *keys, attention, text_rows, 8, groups
     )
     attention = attention.reshape(tiles * 2, groups, rows, head_dim)
     back = lax.all_to_all(attention, ("row", "col"), 0, 0, tiled=True)

time: 118 us -> 119 us (level)
  no operation moved by 1% of the time
where the time goes in v5:
time: 119 us; the launch traced here: 118 us
  waiting for transfers between devices  55.6 us (47%)
  Pallas kernels  42.9 us (36%)
  starting transfers between devices  17 us (14%)
  local copies, waits for them, and re-layouts  1.72 us (1%)
    all_to_all x2, waiting for transfers between devices, exchange(): return lax.all_to_all(mixed, 'row', 0, 0, tiled=True)  35.3 us
    all_to_all x1, waiting for transfers between devices, per_device(): back = lax.all_to_all(attention, ('row', 'col'), 0, 0, tiled=True)  18.7 us
    pallas_call x3, Pallas kernels, qkv_heads(): pl.pallas_call(functools.partial(qkv_kernel, sides=sides, jobs=jobs, samp...  17.9 us
    pallas_call x2, Pallas kernels, attend(): pl.pallas_call(functools.partial(attend_kernel, arrays=len(packed), heads...  12.3 us
    all_to_all x2, starting transfers between devices, exchange(): return lax.all_to_all(mixed, 'row', 0, 0, tiled=True)  12.3 us
    pallas_call x1, Pallas kernels, finish(): pl.pallas_call(finish_kernel, in_specs=[near, far, far, near, near, far,...  8.96 us
    all_to_all x1, starting transfers between devices, per_device(): back = lax.all_to_all(attention, ('row', 'col'), 0, 0, tiled=True)  4.35 us
    pallas_call x1, Pallas kernels, norm_tokens(): pl.pallas_call(norm_kernel, in_specs=[in_place()] * 5, out_specs=[in_vmem...  3.7 us
  transfers between devices with their start and end apart: 5, of which 4 were waited for; matrix products, arithmetic and copies ran while one was open for 0% of the time, Pallas kernels for 23%

profile of v5, /device:TPU:0, one launch (start us, length us, event | category | flops | bytes accessed | tf_op | source)
XLA Modules:
  0.0 118.2 jit_solution(12095283902834207545)
XLA Ops:
  0.6 0.0 copy-start.4
  0.6 0.0 copy-start.5
  0.7 3.7 %norm_tokens.1 = (bf16[400,3072]{1,0:T(8,128)(2,1)S(1)}, bf16[3072,768]{1,0:T(8,128)(2,1)S(1)}) custom-call(bf16[8,16,3072]{2,1,0:T(8,128)(2,1)} %text.1, bf16[8,32,3072]{2,1,0:T(8,128)(2,1)} %img.1, f32[5,8,3072]{2,1,0:T(8,128)} %bitcast.18, bf16[3,3072,768]{2,1,0:T(8,128)(2,1)} %bitcast.10, s32[3,32]{1,0:T(4,128)} %bitcast.22), custom_call_target="tpu_custom_call" | custom-call | flops 11796480 | bytes 4718592 | tf_op jit(solution)/shard_map/norm_tokens/pallas_call | solution.py:113
  4.4 0.1 collective-permute-start
  4.5 0.0 copy-done.4
  4.5 0.0 copy-done.5
  4.5 3.1 %qkv_heads.4.refs_5_ = bf16[8,2,6,48,128]{4,3,2,1,0:T(8,128)(2,1)} custom-call(bf16[400,3072]{1,0:T(8,128)(2,1)S(1)} %get-tuple-element.8.refs_0_, bf16[3,3072,768]{2,1,0:T(8,128)(2,1)} %bitcast.11, f32[8,128]{1,0:T(8,128)S(1)} %copy-done.4, f32[2,128]{1,0:T(2,128)S(1)} %copy-done.5, bf16[3072,768]{1,0:T(8,128)(2,1)S(1)} %get-tuple-element.9.refs_4_), custom_call_target="tpu_custom_call" | custom-call | flops 1811939328 | bytes 7077888 | tf_op jit(solution)/shard_map/qkv_heads/pallas_call | solution.py:218
  7.6 1.5 %collective-permute-done.refs_1_.refs_0_ = bf16[400,3072]{1,0:T(8,128)(2,1)S(1)} collective-permute-done((bf16[400,3072]{1,0:T(8,128)(2,1)S(1)}, bf16[400,3072]{1,0:T(8,128)(2,1)S(1)}, u32[]{:S(2)}, u32[]{:S(2)}) %collective-permute-start) | collective-permute-done | bytes 2457632 | tf_op jit(solution)/shard_map/ppermute | solution.py:452
  9.1 0.0 copy-start.2
  9.1 3.1 %qkv_heads.5 = bf16[8,2,6,48,128]{4,3,2,1,0:T(8,128)(2,1)} custom-call(bf16[400,3072]{1,0:T(8,128)(2,1)S(1)} %collective-permute-done.refs_1_.refs_0_, bf16[3,3072,768]{2,1,0:T(8,128)(2,1)} %bitcast.12, f32[8,128]{1,0:T(8,128)S(1)} %copy-done.4, f32[2,128]{1,0:T(2,128)S(1)} %copy-done.5, ...), custom_call_target="tpu_custom_call", output_to_operand_aliasing={{}: (5, {})} | custom-call | flops 1811939328 | bytes 7077888 | tf_op jit(solution)/shard_map/qkv_heads/pallas_call | solution.py:218
  12.2 0.0 copy-done.2
  12.2 8.2 %all-to-all-start.1 = ((bf16[16,6,48,128]{3,2,1,0:T(8,128)(2,1)}), bf16[16,6,48,128]{3,2,1,0:T(8,128)(2,1)}, u32[]{:S(2)}, u32[]{:S(2)}) async-start(bf16[16,6,48,128]{3,2,1,0:T(8,128)(2,1)} %bitcast.14), calls=%async_computation.1 | async-start | bytes 2359296 | tf_op jit(solution)/shard_map/all_to_all | solution.py:457
  20.4 0.3 collective-permute-start.1
  20.7 0.0 copy-start.3
  20.7 1.7 %copy-done.3 = bf16[400,3072]{1,0:T(8,128)(2,1)S(1)} copy-done((bf16[400,3072]{1,0:T(8,128)(2,1)S(1)}, bf16[400,3072]{1,0:T(8,128)(2,1)}, u32[]{:S(2)}) %copy-start.3) | copy-done | bytes 2457624
  22.4 11.7 %qkv_heads.3 = bf16[8,2,12,48,128]{4,3,2,1,0:T(8,128)(2,1)} custom-call(bf16[400,3072]{1,0:T(8,128)(2,1)S(1)} %get-tuple-element.8.refs_0_, bf16[400,3072]{1,0:T(8,128)(2,1)S(1)} %copy-done.3, bf16[3,3072,768]{2,1,0:T(8,128)(2,1)} %bitcast.13, f32[8,128]{1,0:T(8,128)S(1)} %copy-done.4, f32[2,128]{1,0:T(2,128)S(1)} %copy-done.5), custom_call_target="tpu_custom_call" | custom-call | flops 7247757312 | bytes 9437184 | tf_op jit(solution)/shard_map/qkv_heads/pallas_call | solution.py:218
  34.1 6.0 %all-to-all-done.1.refs_2_ = bf16[16,6,48,128]{3,2,1,0:T(8,128)(2,1)} async-done(((bf16[16,6,48,128]{3,2,1,0:T(8,128)(2,1)}), bf16[16,6,48,128]{3,2,1,0:T(8,128)(2,1)}, u32[]{:S(2)}, u32[]{:S(2)}) %all-to-all-start.1) | async-done | bytes 1179680 | tf_op jit(solution)/shard_map/all_to_all | solution.py:457
  40.2 0.0 copy-start.6
  40.2 4.1 %all-to-all-start = ((bf16[16,12,48,128]{3,2,1,0:T(8,128)(2,1)}), bf16[16,12,48,128]{3,2,1,0:T(8,128)(2,1)S(1)}, u32[]{:S(2)}, u32[]{:S(2)}) async-start(bf16[16,12,48,128]{3,2,1,0:T(8,128)(2,1)} %bitcast.17), calls=%async_computation | async-start | bytes 4718592 | tf_op jit(solution)/shard_map/all_to_all | solution.py:457
  44.2 0.0 copy-done.6
  44.3 0.0 copy-done.7
  44.3 5.1 %attend.2.refs_3_ = bf16[16,2,3,48,128]{4,3,2,1,0:T(8,128)(2,1)} custom-call(s32[8]{0:T(128)S(1)} %copy-done.7, s32[8,16]{1,0:T(8,128)S(1)} %copy-done.6, bf16[16,6,48,128]{3,2,1,0:T(8,128)(2,1)} %all-to-all-done.1.refs_2_), custom_call_target="tpu_custom_call" | custom-call | flops 2415919104 | bytes 1572864 | tf_op jit(solution)/shard_map/attend/pallas_call | solution.py:298
  49.4 29.3 %all-to-all-done.refs_2_ = bf16[16,12,48,128]{3,2,1,0:T(8,128)(2,1)S(1)} async-done(((bf16[16,12,48,128]{3,2,1,0:T(8,128)(2,1)}), bf16[16,12,48,128]{3,2,1,0:T(8,128)(2,1)S(1)}, u32[]{:S(2)}, u32[]{:S(2)}) %all-to-all-start) | async-done | bytes 2359328 | tf_op jit(solution)/shard_map/all_to_all | solution.py:457
  78.7 7.2 %attend.3 = bf16[16,2,3,48,128]{4,3,2,1,0:T(8,128)(2,1)} custom-call(s32[8]{0:T(128)S(1)} %copy-done.7, s32[8,16]{1,0:T(8,128)S(1)} %copy-done.6, bf16[16,12,48,128]{3,2,1,0:T(8,128)(2,1)S(1)} %all-to-all-done.refs_2_, bf16[16,2,3,48,128]{4,3,2,1,0:T(8,128)(2,1)} %attend.2.refs_3_), custom_call_target="tpu_custom_call", output_to_operand_aliasing={{}: (3, {})} | custom-call | flops 4831838208 | bytes 3145728 | tf_op jit(solution)/shard_map/attend/pallas_call | solution.py:298
  85.9 0.0 copy-start
  85.9 0.0 copy-start.1
  85.9 4.3 %all-to-all-start.2 = ((bf16[32,3,48,128]{3,2,1,0:T(8,128)(2,1)}), bf16[32,3,48,128]{3,2,1,0:T(8,128)(2,1)S(1)}, u32[]{:S(2)}, u32[]{:S(2)}) async-start(bf16[32,3,48,128]{3,2,1,0:T(8,128)(2,1)} %bitcast.20), calls=%async_computation.2 | async-start | bytes 2359296 | tf_op jit(solution)/shard_map/all_to_all | solution.py:482
  90.3 0.0 collective-permute-done.1.other_w
  90.3 18.7 %all-to-all-done.2 = bf16[32,3,48,128]{3,2,1,0:T(8,128)(2,1)S(1)} async-done(((bf16[32,3,48,128]{3,2,1,0:T(8,128)(2,1)}), bf16[32,3,48,128]{3,2,1,0:T(8,128)(2,1)S(1)}, u32[]{:S(2)}, u32[]{:S(2)}) %all-to-all-start.2) | async-done | bytes 1179680 | tf_op jit(solution)/shard_map/all_to_all | solution.py:482
  109.0 0.0 copy-done
  109.0 0.0 copy-done.1
  109.0 9.0 %finish.1 = (bf16[8,16,3072]{2,1,0:T(8,128)(2,1)}, bf16[8,32,3072]{2,1,0:T(8,128)(2,1)}, f32[8,32,64]{2,1,0:T(8,128)}) custom-call(bf16[8,2,2,3,48,128]{5,4,3,2,1,0:T(8,128)(2,1)S(1)} %bitcast.9, bf16[3,2,128,3072]{3,2,1,0:T(8,128)(2,1)} %bitcast.16, bf16[3,2,128,3072]{3,2,1,0:T(8,128)(2,1)} %collective-permute-done.1.other_w, ...), custom_call_target="tpu_custom_call" | custom-call | flops 3623878656 | bytes 9437184 | tf_op jit(solution)/shard_map/finish/pallas_call | solution.py:393
  (1 shorter events, 0.0 us)
Async XLA Ops:
  0.6 3.8 %copy-start.4 = (f32[8,128]{1,0:T(8,128)S(1)}, f32[8,128]{1,0:T(8,128)}, u32[]{:S(2)}) copy-start(f32[8,128]{1,0:T(8,128)} %constant.2.clone.refs_3_.refs_2_) | copy-start | bytes 12292
  0.6 3.8 %copy-start.5 = (f32[2,128]{1,0:T(2,128)S(1)}, f32[2,128]{1,0:T(2,128)}, u32[]{:S(2)}) copy-start(f32[2,128]{1,0:T(2,128)} %refs_3_.4) | copy-start | bytes 3076
  4.4 4.8 %collective-permute-start = (bf16[400,3072]{1,0:T(8,128)(2,1)S(1)}, bf16[400,3072]{1,0:T(8,128)(2,1)S(1)}, u32[]{:S(2)}, u32[]{:S(2)}) collective-permute-start(bf16[400,3072]{1,0:T(8,128)(2,1)S(1)} %get-tuple-element.8.refs_0_), channel_id=1, source_target_pairs={{0,1},{1,0},{2,3},{3,2},{4,5},{5,4},{6,7},{7,6},{8,9},{9,8},{10,11... | collective-permute-start | bytes 7372808 | tf_op jit(solution)/shard_map/ppermute | solution.py:452
  9.1 3.1 %copy-start.2 = (bf16[400,3072]{1,0:T(8,128)(2,1)}, bf16[400,3072]{1,0:T(8,128)(2,1)S(1)}, u32[]{:S(2)}) copy-start(bf16[400,3072]{1,0:T(8,128)(2,1)S(1)} %collective-permute-done.refs_1_.refs_0_) | copy-start | bytes 7372804
  12.2 27.9 %all-to-all-start.1 = ((bf16[16,6,48,128]{3,2,1,0:T(8,128)(2,1)}), bf16[16,6,48,128]{3,2,1,0:T(8,128)(2,1)}, u32[]{:S(2)}, u32[]{:S(2)}) async-start(bf16[16,6,48,128]{3,2,1,0:T(8,128)(2,1)} %bitcast.14), calls=%async_computation.1 | async-start | bytes 2359296 | tf_op jit(solution)/shard_map/all_to_all | solution.py:457
  20.4 69.8 %collective-permute-start.1 = (bf16[3,2,128,3072]{3,2,1,0:T(8,128)(2,1)}, bf16[3,2,128,3072]{3,2,1,0:T(8,128)(2,1)}, u32[]{:S(2)}, u32[]{:S(2)}) collective-permute-start(bf16[3,2,128,3072]{3,2,1,0:T(8,128)(2,1)} %bitcast.15), channel_id=1, source_target_pairs={{0,1},{1,0},{2,3},{3,2},{4,5},{5,4},{6,7},{7,6},{8,9},{9,8},{10,11... | collective-permute-start | bytes 14155784 | tf_op jit(solution)/shard_map/ppermute | solution.py:453
  20.7 1.7 %copy-start.3 = (bf16[400,3072]{1,0:T(8,128)(2,1)S(1)}, bf16[400,3072]{1,0:T(8,128)(2,1)}, u32[]{:S(2)}) copy-start(bf16[400,3072]{1,0:T(8,128)(2,1)} %copy-done.2) | copy-start | bytes 7372804
  40.2 4.1 %copy-start.6 = (s32[8,16]{1,0:T(8,128)S(1)}, s32[8,16]{1,0:T(8,128)}, u32[]{:S(2)}) copy-start(s32[8,16]{1,0:T(8,128)} %refs_1_.3) | copy-start | bytes 1540
  40.2 4.1 %copy-start.7 = (s32[8]{0:T(128)S(1)}, s32[8]{0:T(128)}, u32[]{:S(2)}) copy-start(s32[8]{0:T(128)} %refs_0_.3) | copy-start | bytes 100
  40.2 38.5 %all-to-all-start = ((bf16[16,12,48,128]{3,2,1,0:T(8,128)(2,1)}), bf16[16,12,48,128]{3,2,1,0:T(8,128)(2,1)S(1)}, u32[]{:S(2)}, u32[]{:S(2)}) async-start(bf16[16,12,48,128]{3,2,1,0:T(8,128)(2,1)} %bitcast.17), calls=%async_computation | async-start | bytes 4718592 | tf_op jit(solution)/shard_map/all_to_all | solution.py:457
  85.9 23.1 %copy-start = (bf16[8,32,3072]{2,1,0:T(8,128)(2,1)S(1)}, bf16[8,32,3072]{2,1,0:T(8,128)(2,1)}, u32[]{:S(2)}) copy-start(bf16[8,32,3072]{2,1,0:T(8,128)(2,1)} %img.1) | copy-start | bytes 4718596
  85.9 23.1 %copy-start.1 = (bf16[8,16,3072]{2,1,0:T(8,128)(2,1)S(1)}, bf16[8,16,3072]{2,1,0:T(8,128)(2,1)}, u32[]{:S(2)}) copy-start(bf16[8,16,3072]{2,1,0:T(8,128)(2,1)} %text.1) | copy-start | bytes 2359300
  85.9 23.1 %all-to-all-start.2 = ((bf16[32,3,48,128]{3,2,1,0:T(8,128)(2,1)}), bf16[32,3,48,128]{3,2,1,0:T(8,128)(2,1)S(1)}, u32[]{:S(2)}, u32[]{:S(2)}) async-start(bf16[32,3,48,128]{3,2,1,0:T(8,128)(2,1)} %bitcast.20), calls=%async_computation.2 | async-start | bytes 2359296 | tf_op jit(solution)/shard_map/all_to_all | solution.py:482
